TPU v7x, 1024 devices: a whole 4x4x32 slice. The times are simulated.
1024 devices in a mesh: section: 4 (over y), dp: 8 (over x, core), expert: 32 (over z).
Axes of the slice: x: 4, y: 4, z: 32, core: 2. Of those that a mesh axis runs over, the one named last changes fastest.
Arguments:
- tokens_in: bfloat16 [4, 32768, 3072], P('section', ('dp', 'expert')), may hold values from -6 to 6
- upstream: bfloat16 [4, 32768, 3072], P('section', ('dp', 'expert')), may hold values from -6 to 6
- routes: int32 [4, 32768, 2], P('section', ('dp', 'expert')), may hold values from 0 to 31, as said below
- combine: bfloat16 [4, 32768, 2], P('section', ('dp', 'expert')), may hold values from 0.099609375 to 0.8984375
- gate_proj: bfloat16 [4, 32, 3072, 128], P('section', 'expert'), may hold values from -0.109375 to 0.109375
- up_proj: bfloat16 [4, 32, 3072, 128], P('section', 'expert'), may hold values from -0.109375 to 0.109375
- down_proj: bfloat16 [4, 32, 3072, 128], P('section', 'expert'), may hold values from -0.5 to 0.5
Outputs:
- prev_grad: bfloat16 [4, 32768, 3072], P('section', ('dp', 'expert'))
- weight_grad: float32 [4, 32, 3072, 384], P('section', 'expert', 'dp')
- combine_grad: bfloat16 [4, 32768, 2], P('section', ('dp', 'expert'))
Inputs may be any that keep to these rules, and one draw needn't show every extreme that they name: `routes`: each token names two different experts. Of the 128 tokens of one device, at most 9 name any one expert, and in every section and replica one expert is named by exactly 9 tokens of every device.
All inputs are finite; a program needn't handle non-finite values.
Results may differ from a plain program's by a relative error of at most 0.012.
Values may be sent and summed in bfloat16 or wider, within the bound.
No kernel may reach another device: no remote copies, remote signals or barrier semaphores. Data moves between devices by JAX's collectives and lax.ppermute only.
A program may use at most 64 MiB of HBM per device.

v0:
```python
import jax
import jax.numpy as jnp
from jax import lax
from jax.sharding import PartitionSpec as P


def sent_together(arrays, axis, split_dim, concat_dim, along):
    columns = [a.reshape(*a.shape[:along], -1) for a in arrays]
    both = jnp.concatenate(columns, axis=along)
    whole, at, done = (
        lax.all_to_all(both, axis, split_axis=split_dim, concat_axis=concat_dim, tiled=True),
        0,
        [],
    )
    for a, column in zip(arrays, columns):
        slab = whole[..., at : at + column.shape[along]]
        done.append(slab.reshape(*slab.shape[:along], *a.shape[along:]))
        at += column.shape[along]
    return tuple(done)


def split_up(x, dim, length):
    dims = x.shape
    pieces = x.reshape(*dims[:dim], length, dims[dim] // length, *dims[dim + 1 :])
    return jnp.moveaxis(pieces, dim, 0)


def cut_rows(length, count):
    unit = 8 if length >= 8 * count else 1
    return [length // unit * k // count * unit for k in range(1, count)]


def in_order(pieces, dim):
    dims = list(pieces.shape[1:])
    dims[dim] *= pieces.shape[0]
    return jnp.moveaxis(pieces, 0, dim).reshape(dims)


def several_exchanges(x, axis, pieces, split_dim, concat_dim):
    blocks = split_up(x, split_dim, lax.axis_size(axis))
    cut = max(range(1, max(2, blocks.ndim - 1)), key=lambda d: blocks.shape[d])
    done = []
    for slab in jnp.split(blocks, cut_rows(blocks.shape[cut], pieces), axis=cut):
        if slab.size:
            done.append(lax.all_to_all(slab, axis, split_axis=0, concat_axis=0, tiled=True))
    return in_order(jnp.concatenate(done, axis=cut), concat_dim)


def summed_on_arrival(x, axis, dim):
    pieces = split_up(x, dim, lax.axis_size(axis))
    arrived = lax.all_to_all(pieces, axis, split_axis=0, concat_axis=0, tiled=True)
    return arrived.astype(jnp.float32).sum(axis=0)


def from_behind(value, axis, steps):
    count = lax.axis_size(axis)
    pairs = [(source, (source + steps) % count) for source in range(count)]
    return lax.ppermute(value, axis, pairs)


def place_slots(chosen, expert_count, capacity):
    assigned = chosen.shape[0]
    onehot = (chosen[:, None] == jnp.arange(expert_count, dtype=jnp.int32)[None, :]).astype(
        jnp.int32
    )
    before = jnp.cumsum(onehot, axis=0) - onehot
    within = jnp.sum(before * onehot, axis=1)
    target = chosen * capacity + within
    filler = jnp.full((expert_count * capacity,), assigned, jnp.int32)
    filler = filler.at[target].set(jnp.arange(assigned, dtype=jnp.int32))
    return (target, filler)


def fill_rows(token_rows, filler):
    padded = jnp.concatenate(
        [token_rows, jnp.zeros((1, token_rows.shape[1]), token_rows.dtype)], axis=0
    )
    return jnp.take(padded, filler // 2, axis=0)


def fill_weights(weight_flat, filler):
    padded = jnp.concatenate([weight_flat, jnp.zeros((1,), weight_flat.dtype)])
    return jnp.take(padded, filler, axis=0)


def move_pair(slot_block, slot_small):
    return sent_together((slot_block, slot_small), "expert", 0, 0, 2)


def move_single(slot_block):
    return several_exchanges(slot_block, "expert", 2, 0, 0)


def per_device(tokens_in, upstream, routes, combine, gate_proj, up_proj, down_proj):
    token_rows = tokens_in[0]
    grad_rows = upstream[0]
    tok_count = token_rows.shape[0]
    model_width = token_rows.shape[1]
    expert_count = lax.axis_size("expert")
    capacity = 9 * tok_count // (4 * expert_count)
    chosen = routes[0].reshape(-1)
    target, filler = place_slots(chosen, expert_count, capacity)
    slot_rows = fill_rows(token_rows, filler).reshape(expert_count, capacity, model_width)
    slot_weights = fill_weights(combine[0].reshape(-1), filler).reshape(expert_count, capacity)
    slot_grads = fill_rows(grad_rows, filler).reshape(expert_count, capacity, model_width)
    arrived_rows, arrived_weights = move_pair(slot_rows, slot_weights)
    arrived_grads = move_single(slot_grads)
    expert_rows = arrived_rows.reshape(-1, model_width)
    expert_grads = arrived_grads.reshape(-1, model_width)
    expert_weights = arrived_weights.reshape(-1)
    gate_w = gate_proj[0, 0]
    up_w = up_proj[0, 0]
    down_w = down_proj[0, 0]
    by_hidden = (((1,), (1,)), ((), ()))
    by_rows = (((0,), (0,)), ((), ()))
    gate = jnp.dot(expert_rows, gate_w, preferred_element_type=jnp.float32)
    upper = jnp.dot(expert_rows, up_w, preferred_element_type=jnp.float32)
    active = jax.nn.silu(gate)
    hidden = (active * upper).astype(jnp.bfloat16)
    output = lax.dot_general(hidden, down_w, by_hidden, preferred_element_type=jnp.float32)
    grads_wide = expert_grads.astype(jnp.float32)
    gate_slot = jnp.sum(output * grads_wide, axis=1).astype(jnp.bfloat16)
    d_output = (expert_weights.astype(jnp.float32)[:, None] * grads_wide).astype(jnp.bfloat16)
    d_hidden = jnp.dot(d_output, down_w, preferred_element_type=jnp.float32)
    sigma = jax.nn.sigmoid(gate)
    d_gate = (d_hidden * upper * (sigma * (1.0 + gate * (1.0 - sigma)))).astype(jnp.bfloat16)
    d_up = (d_hidden * active).astype(jnp.bfloat16)
    slot_grad = lax.dot_general(d_gate, gate_w, by_hidden, preferred_element_type=jnp.float32)
    slot_grad = slot_grad + lax.dot_general(
        d_up, up_w, by_hidden, preferred_element_type=jnp.float32
    )
    slot_grad = slot_grad.astype(jnp.bfloat16)
    returned_grad, returned_gate = move_pair(
        slot_grad.reshape(expert_count, capacity, model_width),
        gate_slot.reshape(expert_count, capacity),
    )
    summed = summed_on_arrival(
        jnp.concatenate(
            [
                lax.dot_general(expert_rows, d_gate, by_rows, preferred_element_type=jnp.float32),
                lax.dot_general(expert_rows, d_up, by_rows, preferred_element_type=jnp.float32),
                lax.dot_general(d_output, hidden, by_rows, preferred_element_type=jnp.float32),
            ],
            axis=1,
        ).astype(jnp.bfloat16),
        "dp",
        0,
    )
    weight_grad = (summed * (1.0 / lax.axis_size("dp")))[None, None]
    picked = jnp.take(returned_grad.reshape(-1, model_width), target, axis=0)
    picked = picked.reshape(tok_count, 2, model_width).astype(jnp.float32)
    token_grad = jnp.sum(picked, axis=1).astype(jnp.bfloat16)
    combine_grad = jnp.take(returned_gate.reshape(-1), target, axis=0).reshape(tok_count, 2)
    prev_grad = from_behind(token_grad[None], "section", -1)
    return (prev_grad, weight_grad, combine_grad[None])


def solution(mesh):
    return jax.shard_map(
        per_device,
        mesh=mesh,
        in_specs=(
            P("section", ("dp", "expert"), None),
            P("section", ("dp", "expert"), None),
            P("section", ("dp", "expert"), None),
            P("section", ("dp", "expert"), None),
            P("section", "expert", None, None),
            P("section", "expert", None, None),
            P("section", "expert", None, None),
        ),
        out_specs=(
            P("section", ("dp", "expert"), None),
            P("section", "expert", "dp", None),
            P("section", ("dp", "expert"), None),
        ),
        check_vma=False,
    )
```

profile of v0, /device:TPU:186, one launch (start us, length us, event | category | flops | bytes accessed | tf_op | source)
XLA Modules:
  0.0 973.9 jit_solution(9734911390002180828)
XLA Ops:
  13.2 3.6 broadcast_select_fusion.2
  21.7 26.8 %all-to-all-start.1 = ((bf16[32,1,4,3072]{3,2,1,0:T(4,128)(2,1)}), bf16[32,1,4,3072]{3,2,1,0:T(4,128)(2,1)S(1)}, u32[]{:S(2)}, u32[]{:S(2)}) async-start(bf16[32,1,4,3072]{3,2,1,0:T(4,128)(2,1)} %slice_bitcast_fusion.1), calls=%async_computation.1 | async-start | bytes 1572864 | tf_op jit(solution)/shard_map/all_to_all | solution.py:45
  48.5 3.6 slice_bitcast_fusion
  52.0 78.2 %all-to-all-done.1 = bf16[32,1,4,3072]{3,2,1,0:T(4,128)(2,1)S(1)} async-done(((bf16[32,1,4,3072]{3,2,1,0:T(4,128)(2,1)}), bf16[32,1,4,3072]{3,2,1,0:T(4,128)(2,1)S(1)}, u32[]{:S(2)}, u32[]{:S(2)}) %all-to-all-start.1) | async-done | bytes 786464 | tf_op jit(solution)/shard_map/all_to_all | solution.py:45
  130.2 9.0 all-to-all-start.2
  139.3 4.2 reshape.213
  146.5 3.9 pad_maximum_fusion
  150.4 137.4 %all-to-all-done.2 = bf16[32,1,5,3072]{3,2,1,0:T(8,128)(2,1)S(1)} async-done(((bf16[32,1,5,3072]{3,2,1,0:T(8,128)(2,1)}), bf16[32,1,5,3072]{3,2,1,0:T(8,128)(2,1)S(1)}, u32[]{:S(2)}, u32[]{:S(2)}) %all-to-all-start.2) | async-done | bytes 983072 | tf_op jit(solution)/shard_map/all_to_all | solution.py:45
  287.9 8.3 all-to-all-start
  296.2 3.8 maximum_convert_fusion
  300.0 5.2 reshape.218
  305.2 286.3 %all-to-all-done = bf16[32,9,3073]{2,1,0:T(8,128)(2,1)} async-done(((bf16[32,9,3073]{2,1,0:T(8,128)(2,1)}), bf16[32,9,3073]{2,1,0:T(8,128)(2,1)}, u32[]{:S(2)}, u32[]{:S(2)}) %all-to-all-start) | async-done | bytes 1770080 | tf_op jit(solution)/shard_map/all_to_all | solution.py:11
  595.9 4.2 convert_element_type.102
  600.2 3.9 slice.36
  613.0 4.2 reshape.215
  620.1 3.9 pad_maximum_fusion.1
  624.0 8.8 all-to-all-start.3
  638.8 289.5 %all-to-all-done.3 = bf16[32,9,3073]{2,1,0:T(8,128)(2,1)} async-done(((bf16[32,9,3073]{2,1,0:T(8,128)(2,1)}), bf16[32,9,3073]{2,1,0:T(8,128)(2,1)}, u32[]{:S(2)}, u32[]{:S(2)}) %all-to-all-start.3) | async-done | bytes 1770080 | tf_op jit(solution)/shard_map/all_to_all | solution.py:11
  928.3 4.8 all-to-all-start.4
  933.7 3.9 slice.37
  943.3 3.5 gather.21
  946.8 3.5 fusion.8
  953.0 8.7 all-to-all-done.4
  968.8 4.2 collective-permute-done
  (91 shorter events, 59.4 us)
Async XLA Ops:
  0.6 606.4 %copy-start = (bf16[1,1,3072,128]{3,2,1,0:T(8,128)(2,1)S(1)}, bf16[1,1,3072,128]{3,2,1,0:T(8,128)(2,1)}, u32[]{:S(2)}) copy-start(bf16[1,1,3072,128]{3,2,1,0:T(8,128)(2,1)} %param.13) | copy-start | bytes 2359300
  0.6 5.7 copy-start.6
  21.7 108.5 %all-to-all-start.1 = ((bf16[32,1,4,3072]{3,2,1,0:T(4,128)(2,1)}), bf16[32,1,4,3072]{3,2,1,0:T(4,128)(2,1)S(1)}, u32[]{:S(2)}, u32[]{:S(2)}) async-start(bf16[32,1,4,3072]{3,2,1,0:T(4,128)(2,1)} %slice_bitcast_fusion.1), calls=%async_computation.1 | async-start | bytes 1572864 | tf_op jit(solution)/shard_map/all_to_all | solution.py:45
  130.2 157.7 %all-to-all-start.2 = ((bf16[32,1,5,3072]{3,2,1,0:T(8,128)(2,1)}), bf16[32,1,5,3072]{3,2,1,0:T(8,128)(2,1)S(1)}, u32[]{:S(2)}, u32[]{:S(2)}) async-start(bf16[32,1,5,3072]{3,2,1,0:T(8,128)(2,1)} %slice_bitcast_fusion), calls=%async_computation.2 | async-start | bytes 3145728 | tf_op jit(solution)/shard_map/all_to_all | solution.py:45
  139.3 4.2 copy-start.10
  287.9 303.6 %all-to-all-start = ((bf16[32,9,3073]{2,1,0:T(8,128)(2,1)}), bf16[32,9,3073]{2,1,0:T(8,128)(2,1)}, u32[]{:S(2)}, u32[]{:S(2)}) async-start(bf16[32,9,3073]{2,1,0:T(8,128)(2,1)} %pad_maximum_fusion), calls=%async_computation | async-start | bytes 6553600 | tf_op jit(solution)/shard_map/all_to_all | solution.py:11
  607.0 1.1 copy-start.3
  608.2 1.5 copy-start.4
  608.2 1.7 copy-start.5
  610.5 0.6 copy-start.7
  624.0 304.2 %all-to-all-start.3 = ((bf16[32,9,3073]{2,1,0:T(8,128)(2,1)}), bf16[32,9,3073]{2,1,0:T(8,128)(2,1)}, u32[]{:S(2)}, u32[]{:S(2)}) async-start(bf16[32,9,3073]{2,1,0:T(8,128)(2,1)} %pad_maximum_fusion.1), calls=%async_computation.3 | async-start | bytes 6553600 | tf_op jit(solution)/shard_map/all_to_all | solution.py:11
  632.8 1.8 copy-start.8
  634.0 2.0 copy-start.2
  638.8 294.6 %copy-start.9 = (s32[1,128,2]{1,2,0:T(2,128)S(1)}, s32[1,128,2]{1,2,0:T(2,128)}, u32[]{:S(2)}) copy-start(s32[1,128,2]{1,2,0:T(2,128)} %param.11) | copy-start | bytes 3076
  928.3 33.5 %all-to-all-start.4 = ((bf16[8,384,384]{1,2,0:T(8,128)(2,1)}), bf16[8,384,384]{1,2,0:T(8,128)(2,1)}, u32[]{:S(2)}, u32[]{:S(2)}) async-start(bf16[8,384,384]{1,2,0:T(8,128)(2,1)} %pad_maximum_fusion.2), calls=%async_computation.4 | async-start | bytes 4718592 | tf_op jit(solution)/shard_map/all_to_all | solution.py:51
  950.3 22.7 %collective-permute-start = (bf16[1,128,3072]{2,1,0:T(8,128)(2,1)S(1)}, bf16[1,128,3072]{2,1,0:T(8,128)(2,1)S(1)}, u32[]{:S(2)}, u32[]{:S(2)}) collective-permute-start(bf16[1,128,3072]{2,1,0:T(8,128)(2,1)S(1)} %bitcast.91), channel_id=1, source_target_pairs={{0,768},{256,0},{512,256},{768,512},{1,769},{257,1},{513,257},{769... | collective-permute-start | bytes 2359304 | tf_op jit(solution)/shard_map/ppermute | solution.py:58
  961.7 12.2 %copy-start.1 = (bf16[1,1,3072,128]{3,2,1,0:T(8,128)(2,1)S(1)}, bf16[1,1,3072,128]{3,2,1,0:T(8,128)(2,1)}, u32[]{:S(2)}) copy-start(bf16[1,1,3072,128]{3,2,1,0:T(8,128)(2,1)} %param.13) | copy-start | bytes 2359300
where the time goes:
time: 975 us; the launch traced here: 974 us
  waiting for transfers between devices  804 us (82%)
  local copies, waits for them, and re-layouts  69 us (7%)
  starting transfers between devices  60.4 us (6%)
  other arithmetic  30.3 us (3%)
    all_to_all x2, waiting for transfers between devices, sent_together(): lax.all_to_all(both, axis, split_axis=split_dim, concat_axis=concat_dim,...  576 us
    all_to_all x2, waiting for transfers between devices, several_exchanges(): lax.all_to_all(slab, axis, split_axis=0, concat_axis=0, tiled=True)  216 us
    all_to_all x2, starting transfers between devices, several_exchanges(): lax.all_to_all(slab, axis, split_axis=0, concat_axis=0, tiled=True)  35.8 us
  transfers between devices with their start and end apart: 6, of which 6 were waited for; matrix products, arithmetic and copies ran while one was open for 5% of the time, Pallas kernels for 0%

commit v1 on v0

v1 whole, which is shorter than its diff:
```python
import jax
import jax.numpy as jnp
from jax import lax
from jax.experimental import pallas as pl
from jax.experimental.pallas import tpu as pltpu
from jax.sharding import PartitionSpec as P


INTERPRET = False
F32 = jnp.float32
BF16 = jnp.bfloat16
SUB = 8
EXTRA = 128


def shifted(value, axis, steps):
    count = lax.axis_size(axis)
    return lax.ppermute(value, axis, [(s, (s + steps) % count) for s in range(count)])


def offsets_of(reach):
    return list(range(-reach, reach + 1))


def blocks_of(d, reach):
    return (d + reach,) if abs(d) == reach else (d + reach, d + 3 * reach)


def selectors(routes_ref, here, experts):
    reach = experts // 4
    tokens = routes_ref.shape[1]
    ids = lax.broadcasted_iota(jnp.int32, (experts, tokens), 0)
    picks = [routes_ref[k : k + 1, :] for k in range(2)]
    named = [jnp.where(ids == p, 1.0, 0.0) for p in picks]
    earlier = lax.broadcasted_iota(jnp.int32, (tokens, tokens), 0) < lax.broadcasted_iota(
        jnp.int32, (tokens, tokens), 1
    )
    before = jnp.dot(
        (named[0] + named[1]).astype(BF16),
        jnp.where(earlier, 1.0, 0.0).astype(BF16),
        preferred_element_type=F32,
    )
    row = lax.broadcasted_iota(jnp.int32, (experts * SUB, tokens), 0)
    main, ninth = [], []
    for p, hit in zip(picks, named):
        slot = jnp.sum(before * hit, axis=0, keepdims=True).astype(jnp.int32)
        block = p - here + reach
        block = jnp.where(block < 0, block + experts, block)
        block = jnp.where(block >= experts, block - experts, block)
        main.append(jnp.where(row == jnp.where(slot < SUB, block * SUB + slot, -1), 1.0, 0.0))
        ninth.append(jnp.where((row >> 3) == jnp.where(slot == SUB, block, -1), 1.0, 0.0))
    return main, ninth, row & (SUB - 1)


def pack_kernel(here_ref, routes_ref, combine_ref, rows_ref, grads_ref, *outs, experts):
    reach = experts // 4
    width = rows_ref.shape[1]
    fold = width // SUB
    main, ninth, sub = selectors(routes_ref, here_ref[0], experts)
    weights = [combine_ref[k : k + 1, :].astype(F32) for k in range(2)]
    for kind, ref in enumerate((rows_ref, grads_ref)):
        if kind == 0:
            pick = main[0] + main[1]
            pick9 = ninth[0] + ninth[1]
        else:
            pick = main[0] * weights[0] + main[1] * weights[1]
            pick9 = ninth[0] * weights[0] + ninth[1] * weights[1]
        body = jnp.dot(pick.astype(BF16), ref[...], preferred_element_type=F32)
        tail = jnp.zeros((experts * SUB, fold), F32)
        for s in range(SUB):
            tail = tail + jnp.dot(
                jnp.where(sub == s, pick9, 0.0).astype(BF16),
                ref[:, s * fold : (s + 1) * fold],
                preferred_element_type=F32,
            )
        for d, out in zip(offsets_of(reach), outs):
            for i, b in enumerate(blocks_of(d, reach)):
                at = slice(b * SUB, (b + 1) * SUB)
                out[2 * i + kind, :, 0:width] = body[at, :].astype(BF16)
                out[2 * i + kind, :, width : width + fold] = tail[at, :].astype(BF16)


def pack(here, routes_t, combine_t, rows, grads, experts):
    reach = experts // 4
    width = rows.shape[1]
    vmem = pl.BlockSpec(memory_space=pltpu.VMEM)
    shapes = [
        jax.ShapeDtypeStruct((2 * len(blocks_of(d, reach)), SUB, width + width // SUB), BF16)
        for d in offsets_of(reach)
    ]
    return pl.pallas_call(
        lambda *refs: pack_kernel(*refs, experts=experts),
        out_shape=shapes,
        in_specs=[pl.BlockSpec(memory_space=pltpu.SMEM)] + [vmem] * 4,
        out_specs=[vmem] * len(shapes),
        name="pack",
        interpret=INTERPRET,
    )(here, routes_t, combine_t, rows, grads)


def gather_blocks(ref_of, count, scratch, folded, width, picks):
    fold = width // SUB
    for b in range(count):
        block = ref_of(b)
        scratch[b * SUB : (b + 1) * SUB, :] = block[:, 0:width]
        folded[b * SUB : (b + 1) * SUB, :] = block[:, width : width + fold]
    whole = folded[0 : count * SUB, :]
    for s in range(SUB):
        nine = jnp.dot(picks[s], whole, preferred_element_type=F32).astype(BF16)
        scratch[count * SUB : count * SUB + nine.shape[0], s * fold : (s + 1) * fold] = nine


def expert_kernel(*refs, experts):
    reach = experts // 4
    offsets = offsets_of(reach)
    arrived = refs[: len(offsets)]
    own_w = refs[len(offsets) : len(offsets) + 3]
    far_w = refs[len(offsets) + 3]
    at = len(offsets) + 4
    returned = refs[at : at + len(offsets)]
    terms = refs[at + len(offsets) : at + len(offsets) + 2]
    x_ref, g_ref, folded = refs[at + len(offsets) + 2 :]
    width = own_w[0].shape[0]
    ff = own_w[0].shape[1]
    fold = width // SUB
    by_hidden = (((1,), (1,)), ((), ()))
    by_rows = (((0,), (0,)), ((), ()))
    for half in range(2):
        reached = reach if half == 0 else reach - 1
        here = [(d, arrived[d + reach]) for d in range(-reached, reached + 1)]
        count = len(here)
        padded = -(-count // SUB) * SUB
        rows = count * SUB + padded
        r0 = lax.broadcasted_iota(jnp.int32, (padded, count * SUB), 0)
        r1 = lax.broadcasted_iota(jnp.int32, (padded, count * SUB), 1)
        picks = [jnp.where(r1 == r0 * SUB + s, 1.0, 0.0).astype(BF16) for s in range(SUB)]
        gather_blocks(lambda b: here[b][1].at[2 * half], count, x_ref, folded, width, picks)
        gather_blocks(lambda b: here[b][1].at[2 * half + 1], count, g_ref, folded, width, picks)
        if half == 0:
            gate_w, up_w, down_w = [w[...] for w in own_w]
        else:
            gate_w, up_w, down_w = [far_w[:, i].reshape(width, ff) for i in range(3)]
        x = x_ref[0:rows, :]
        g = g_ref[0:rows, :]
        gate = jnp.dot(x, gate_w, preferred_element_type=F32)
        upper = jnp.dot(x, up_w, preferred_element_type=F32)
        d_hidden = jnp.dot(g, down_w, preferred_element_type=F32)
        sigma = jax.nn.sigmoid(gate)
        active = gate * sigma
        hidden = (active * upper).astype(BF16)
        weighed = jnp.sum(hidden.astype(F32) * d_hidden, axis=1, keepdims=True)
        d_gate = (d_hidden * upper * (sigma * (1.0 + gate * (1.0 - sigma)))).astype(BF16)
        d_up = (d_hidden * active).astype(BF16)
        slot_grad = lax.dot_general(d_gate, gate_w, by_hidden, preferred_element_type=F32)
        slot_grad = slot_grad + lax.dot_general(d_up, up_w, by_hidden, preferred_element_type=F32)
        nine = slot_grad[count * SUB :, :].astype(BF16)
        q0 = lax.broadcasted_iota(jnp.int32, (count * SUB, padded), 0)
        q1 = lax.broadcasted_iota(jnp.int32, (count * SUB, padded), 1)
        tail = jnp.zeros((count * SUB, fold), F32)
        spread = []
        for s in range(SUB):
            put = jnp.where(q0 == q1 * SUB + s, 1.0, 0.0).astype(BF16)
            spread.append(put)
            tail = tail + jnp.dot(put, nine[:, s * fold : (s + 1) * fold], preferred_element_type=F32)
        nine_sum = jnp.broadcast_to(weighed[count * SUB :, :], (padded, EXTRA)).astype(BF16)
        nine_sum = jnp.dot(spread[0], nine_sum, preferred_element_type=F32)
        lane = lax.broadcasted_iota(jnp.int32, (count * SUB, EXTRA), 1)
        extra = jnp.where(lane == 0, weighed[0 : count * SUB, :], jnp.where(lane == 1, nine_sum, 0.0))
        for b, (d, _) in enumerate(here):
            out = returned[d + reach]
            span = slice(b * SUB, (b + 1) * SUB)
            out[half, :, 0:width] = slot_grad[span, :].astype(BF16)
            out[half, :, width : width + fold] = tail[span, :].astype(BF16)
            out[half, :, width + fold : width + fold + EXTRA] = extra[span, :].astype(BF16)
        term = terms[half]
        term[:, 0:ff] = lax.dot_general(x, d_gate, by_rows, preferred_element_type=F32).astype(BF16)
        term[:, ff : 2 * ff] = lax.dot_general(x, d_up, by_rows, preferred_element_type=F32).astype(
            BF16
        )
        term[:, 2 * ff : 3 * ff] = lax.dot_general(
            g, hidden, by_rows, preferred_element_type=F32
        ).astype(BF16)


def run_experts(arrived, own_w, far_w, experts):
    reach = experts // 4
    width, ff = own_w[0].shape
    fold = width // SUB
    vmem = pl.BlockSpec(memory_space=pltpu.VMEM)
    shapes = [
        jax.ShapeDtypeStruct((len(blocks_of(d, reach)), SUB, width + fold + EXTRA), BF16)
        for d in offsets_of(reach)
    ] + [jax.ShapeDtypeStruct((width, 3 * ff), BF16)] * 2
    count = 2 * reach + 1
    rows = count * SUB + -(-count // SUB) * SUB
    outs = pl.pallas_call(
        lambda *refs: expert_kernel(*refs, experts=experts),
        out_shape=shapes,
        in_specs=[vmem] * (len(arrived) + 4),
        out_specs=[vmem] * len(shapes),
        scratch_shapes=[
            pltpu.VMEM((rows, width), BF16),
            pltpu.VMEM((rows, width), BF16),
            pltpu.VMEM((count * SUB, fold), BF16),
        ],
        name="experts",
        interpret=INTERPRET,
    )(*arrived, *own_w, far_w)
    return outs[:-2], outs[-2], outs[-1]


def unpack_kernel(here_ref, routes_ref, combine_ref, *refs, experts):
    reach = experts // 4
    offsets = offsets_of(reach)
    arrived = refs[: len(offsets)]
    grad_out, combine_out, body, tail, extra = refs[len(offsets) :]
    width = body.shape[1]
    fold = tail.shape[1]
    for d, ref in zip(offsets, arrived):
        for i, b in enumerate(blocks_of(d, reach)):
            span = slice(b * SUB, (b + 1) * SUB)
            body[span, :] = ref[i, :, 0:width]
            tail[span, :] = ref[i, :, width : width + fold]
            extra[span, :] = ref[i, :, width + fold : width + fold + EXTRA].astype(F32)
    main, ninth, sub = selectors(routes_ref, here_ref[0], experts)
    pick = (main[0] + main[1]).T.astype(BF16)
    nine = ninth[0] + ninth[1]
    for s in range(SUB):
        cols = slice(s * fold, (s + 1) * fold)
        total = jnp.dot(pick, body[:, cols], preferred_element_type=F32)
        total = total + jnp.dot(
            jnp.where(sub == s, nine, 0.0).T.astype(BF16), tail[...], preferred_element_type=F32
        )
        grad_out[:, cols] = total.astype(BF16)
    for k in range(2):
        value = main[k] * extra[:, 0:1] + jnp.where(sub == 0, ninth[k], 0.0) * extra[:, 1:2]
        value = jnp.sum(value, axis=0, keepdims=True)
        combine_out[k : k + 1, :] = value / combine_ref[k : k + 1, :].astype(F32)


def unpack(here, routes_t, combine_t, arrived, width, experts):
    tokens = routes_t.shape[1]
    vmem = pl.BlockSpec(memory_space=pltpu.VMEM)
    return pl.pallas_call(
        lambda *refs: unpack_kernel(*refs, experts=experts),
        out_shape=[
            jax.ShapeDtypeStruct((tokens, width), BF16),
            jax.ShapeDtypeStruct((2, tokens), F32),
        ],
        in_specs=[pl.BlockSpec(memory_space=pltpu.SMEM)] + [vmem] * (2 + len(arrived)),
        out_specs=[vmem] * 2,
        scratch_shapes=[
            pltpu.VMEM((experts * SUB, width), BF16),
            pltpu.VMEM((experts * SUB, width // SUB), BF16),
            pltpu.VMEM((experts * SUB, EXTRA), F32),
        ],
        name="unpack",
        interpret=INTERPRET,
    )(here, routes_t, combine_t, *arrived)


def spread_over(x, axis):
    copies = jnp.broadcast_to(x[None], (lax.axis_size(axis),) + x.shape)
    return lax.all_to_all(copies, axis, split_axis=0, concat_axis=0, tiled=True)


def summed_on_arrival(term, axis):
    count = lax.axis_size(axis)
    pieces = term.reshape(count, term.shape[0] // count, term.shape[1])
    arrived = lax.all_to_all(pieces, axis, split_axis=0, concat_axis=0, tiled=True)
    return arrived.astype(F32).sum(axis=0)


def per_device(tokens_in, upstream, routes, combine, gate_proj, up_proj, down_proj):
    experts = lax.axis_size("expert")
    replicas = lax.axis_size("dp")
    reach = experts // 4
    width = tokens_in.shape[2]
    assert 9 * tokens_in.shape[1] == 4 * experts * (SUB + 1)
    here = lax.axis_index("expert").astype(jnp.int32).reshape(1)
    routes_t = routes[0].T
    combine_t = combine[0].T
    own_w = [w[0, 0] for w in (gate_proj, up_proj, down_proj)]
    part = width // replicas
    start = lax.axis_index("dp") * part
    offsets = offsets_of(reach)
    piece = jnp.stack([lax.dynamic_slice_in_dim(w, start, part, 0) for w in own_w])
    piece = shifted(piece, "expert", 2 * reach)
    far_w = spread_over(piece, "dp")
    packed = pack(here, routes_t, combine_t, tokens_in[0], upstream[0], experts)
    arrived = list(packed)
    for i, d in enumerate(offsets):
        if d:
            arrived[i] = shifted(packed[i], "expert", d)
    done, own_term, far_term = run_experts(arrived, own_w, far_w, experts)
    back = list(done)
    for i, d in enumerate(offsets):
        if d:
            back[i] = shifted(done[i], "expert", -d)
    far_sum = summed_on_arrival(far_term, "dp").astype(BF16)
    far_sum = shifted(far_sum, "expert", 2 * reach)
    own_sum = summed_on_arrival(own_term, "dp")
    weight_grad = (own_sum + far_sum.astype(F32)) * (1.0 / replicas)
    token_grad, combine_grad = unpack(here, routes_t, combine_t, back, width, experts)
    prev_grad = shifted(token_grad[None], "section", -1)
    return prev_grad, weight_grad[None, None], combine_grad.astype(BF16).T[None]


def solution(mesh):
    rows = P("section", ("dp", "expert"), None)
    weights = P("section", "expert", None, None)

    return jax.shard_map(
        per_device,
        mesh=mesh,
        in_specs=(rows, rows, rows, rows, weights, weights, weights),
        out_specs=(rows, P("section", "expert", "dp", None), rows),
        check_vma=False,
    )
```

time: 975 us -> 644 us (0.66)
  the two profiles are of different devices: /device:TPU:186 before, /device:TPU:147 now
where the time goes in v1:
time: 644 us; the launch traced here: 643 us
  waiting for transfers between devices  318 us (49%)
  starting transfers between devices  255 us (40%)
  blocking collectives  34.9 us (5%)
  Pallas kernels  20.7 us (3%)
  local copies, waits for them, and re-layouts  6.85 us (1%)
    ppermute x35, waiting for transfers between devices, shifted(): lax.ppermute(value, axis, [(s, (s + steps) % count) for s in range(count)])  318 us
    ppermute x35, starting transfers between devices, shifted(): lax.ppermute(value, axis, [(s, (s + steps) % count) for s in range(count)])  244 us
    all_to_all x1, blocking collectives, summed_on_arrival(): lax.all_to_all(pieces, axis, split_axis=0, concat_axis=0, tiled=True)  34.9 us
  transfers between devices with their start and end apart: 37, of which 20 were waited for; matrix products, arithmetic and copies ran while one was open for 0% of the time, Pallas kernels for 1%

profile of v1, /device:TPU:147, one launch (start us, length us, event | category | flops | bytes accessed | tf_op | source)
XLA Modules:
  0.0 642.5 jit_solution(15952414562139893894)
XLA Ops:
  2.5 23.9 %collective-permute-start.16 = (bf16[3,384,128]{2,1,0:T(8,128)(2,1)S(1)}, bf16[3,384,128]{2,1,0:T(8,128)(2,1)S(1)}, u32[]{:S(2)}, u32[]{:S(2)}) collective-permute-start(bf16[3,384,128]{2,1,0:T(8,128)(2,1)S(1)} %pad_maximum_fusion), channel_id=1, source_target_pairs={{0,16},{1,17},{2,18},{3,19},{4,20},{5,21},{6,22},{7,23},{8,24},{9,... | collective-permute-start | bytes 884744 | tf_op jit(solution)/shard_map/ppermute | solution.py:18
  26.4 27.0 %collective-permute-done.16 = bf16[3,384,128]{2,1,0:T(8,128)(2,1)S(1)} collective-permute-done((bf16[3,384,128]{2,1,0:T(8,128)(2,1)S(1)}, bf16[3,384,128]{2,1,0:T(8,128)(2,1)S(1)}, u32[]{:S(2)}, u32[]{:S(2)}) %collective-permute-start.16) | collective-permute-done | bytes 294944 | tf_op jit(solution)/shard_map/ppermute | solution.py:18
  66.4 31.0 %collective-permute-start = (bf16[2,8,3456]{2,1,0:T(8,128)(2,1)}, bf16[2,8,3456]{2,1,0:T(8,128)(2,1)S(1)}, u32[]{:S(2)}, u32[]{:S(2)}) collective-permute-start(bf16[2,8,3456]{2,1,0:T(8,128)(2,1)} %get-tuple-element.41), channel_id=1, source_target_pairs={{0,24},{1,25},{2,26},{3,27},{4,28},{5,29},{6,30},{7,31},{8,0},{9,1... | collective-permute-start | bytes 331784 | tf_op jit(solution)/shard_map/ppermute | solution.py:18
  108.7 11.6 %collective-permute-start.3 = (bf16[4,8,3456]{2,1,0:T(8,128)(2,1)}, bf16[4,8,3456]{2,1,0:T(8,128)(2,1)S(1)}, u32[]{:S(2)}, u32[]{:S(2)}) collective-permute-start(bf16[4,8,3456]{2,1,0:T(8,128)(2,1)} %get-tuple-element.44), channel_id=1, source_target_pairs={{0,27},{1,28},{2,29},{3,30},{4,31},{5,0},{6,1},{7,2},{8,3},{9,4},{... | collective-permute-start | bytes 663560 | tf_op jit(solution)/shard_map/ppermute | solution.py:18
  122.2 11.9 %collective-permute-done.refs_0_ = bf16[2,8,3456]{2,1,0:T(8,128)(2,1)S(1)} collective-permute-done((bf16[2,8,3456]{2,1,0:T(8,128)(2,1)}, bf16[2,8,3456]{2,1,0:T(8,128)(2,1)S(1)}, u32[]{:S(2)}, u32[]{:S(2)}) %collective-permute-start) | collective-permute-done | bytes 110624 | tf_op jit(solution)/shard_map/ppermute | solution.py:18
  136.0 15.4 %collective-permute-done.15.refs_16_ = bf16[2,8,3456]{2,1,0:T(8,128)(2,1)S(1)} collective-permute-done((bf16[2,8,3456]{2,1,0:T(8,128)(2,1)}, bf16[2,8,3456]{2,1,0:T(8,128)(2,1)S(1)}, u32[]{:S(2)}, u32[]{:S(2)}) %collective-permute-start.15) | collective-permute-done | bytes 110624 | tf_op jit(solution)/shard_map/ppermute | solution.py:18
  158.4 17.8 %collective-permute-start.6 = (bf16[4,8,3456]{2,1,0:T(8,128)(2,1)}, bf16[4,8,3456]{2,1,0:T(8,128)(2,1)S(1)}, u32[]{:S(2)}, u32[]{:S(2)}) collective-permute-start(bf16[4,8,3456]{2,1,0:T(8,128)(2,1)} %get-tuple-element.47), channel_id=1, source_target_pairs={{0,30},{1,31},{2,0},{3,1},{4,2},{5,3},{6,4},{7,5},{8,6},{9,7},{10,... | collective-permute-start | bytes 663560 | tf_op jit(solution)/shard_map/ppermute | solution.py:18
  178.1 17.3 %collective-permute-done.3.refs_3_ = bf16[4,8,3456]{2,1,0:T(8,128)(2,1)S(1)} collective-permute-done((bf16[4,8,3456]{2,1,0:T(8,128)(2,1)}, bf16[4,8,3456]{2,1,0:T(8,128)(2,1)S(1)}, u32[]{:S(2)}, u32[]{:S(2)}) %collective-permute-start.3) | collective-permute-done | bytes 221216 | tf_op jit(solution)/shard_map/ppermute | solution.py:18
  197.4 21.4 %collective-permute-done.4.refs_4_ = bf16[4,8,3456]{2,1,0:T(8,128)(2,1)S(1)} collective-permute-done((bf16[4,8,3456]{2,1,0:T(8,128)(2,1)}, bf16[4,8,3456]{2,1,0:T(8,128)(2,1)S(1)}, u32[]{:S(2)}, u32[]{:S(2)}) %collective-permute-start.4) | collective-permute-done | bytes 221216 | tf_op jit(solution)/shard_map/ppermute | solution.py:18
  220.7 8.7 %collective-permute-start.10 = (bf16[4,8,3456]{2,1,0:T(8,128)(2,1)}, bf16[4,8,3456]{2,1,0:T(8,128)(2,1)S(1)}, u32[]{:S(2)}, u32[]{:S(2)}) collective-permute-start(bf16[4,8,3456]{2,1,0:T(8,128)(2,1)} %get-tuple-element.52), channel_id=1, source_target_pairs={{0,3},{1,4},{2,5},{3,6},{4,7},{5,8},{6,9},{7,10},{8,11},{9,12},{10... | collective-permute-start | bytes 663560 | tf_op jit(solution)/shard_map/ppermute | solution.py:18
  229.4 10.1 %collective-permute-done.6.refs_6_ = bf16[4,8,3456]{2,1,0:T(8,128)(2,1)S(1)} collective-permute-done((bf16[4,8,3456]{2,1,0:T(8,128)(2,1)}, bf16[4,8,3456]{2,1,0:T(8,128)(2,1)S(1)}, u32[]{:S(2)}, u32[]{:S(2)}) %collective-permute-start.6) | collective-permute-done | bytes 221216 | tf_op jit(solution)/shard_map/ppermute | solution.py:18
  247.4 12.6 %collective-permute-start.13 = (bf16[4,8,3456]{2,1,0:T(8,128)(2,1)}, bf16[4,8,3456]{2,1,0:T(8,128)(2,1)S(1)}, u32[]{:S(2)}, u32[]{:S(2)}) collective-permute-start(bf16[4,8,3456]{2,1,0:T(8,128)(2,1)} %get-tuple-element.55), channel_id=1, source_target_pairs={{0,6},{1,7},{2,8},{3,9},{4,10},{5,11},{6,12},{7,13},{8,14},{9,15},... | collective-permute-start | bytes 663560 | tf_op jit(solution)/shard_map/ppermute | solution.py:18
  266.7 22.0 %collective-permute-done.12.refs_13_ = bf16[4,8,3456]{2,1,0:T(8,128)(2,1)S(1)} collective-permute-done((bf16[4,8,3456]{2,1,0:T(8,128)(2,1)}, bf16[4,8,3456]{2,1,0:T(8,128)(2,1)S(1)}, u32[]{:S(2)}, u32[]{:S(2)}) %collective-permute-start.12) | collective-permute-done | bytes 221216 | tf_op jit(solution)/shard_map/ppermute | solution.py:18
  288.8 31.3 %collective-permute-done.13.refs_14_ = bf16[4,8,3456]{2,1,0:T(8,128)(2,1)S(1)} collective-permute-done((bf16[4,8,3456]{2,1,0:T(8,128)(2,1)}, bf16[4,8,3456]{2,1,0:T(8,128)(2,1)S(1)}, u32[]{:S(2)}, u32[]{:S(2)}) %collective-permute-start.13) | collective-permute-done | bytes 221216 | tf_op jit(solution)/shard_map/ppermute | solution.py:18
  320.8 36.0 %collective-permute-done.14.refs_15_ = bf16[4,8,3456]{2,1,0:T(8,128)(2,1)} collective-permute-done((bf16[4,8,3456]{2,1,0:T(8,128)(2,1)}, bf16[4,8,3456]{2,1,0:T(8,128)(2,1)}, u32[]{:S(2)}, u32[]{:S(2)}) %collective-permute-start.14) | collective-permute-done | bytes 221216 | tf_op jit(solution)/shard_map/ppermute | solution.py:18
  358.3 12.2 %experts.1 = (bf16[1,8,3584]{2,1,0:T(8,128)(2,1)}, bf16[2,8,3584]{2,1,0:T(8,128)(2,1)}, bf16[2,8,3584]{2,1,0:T(8,128)(2,1)}, bf16[2,8,3584]{2,1,0:T(8,128)(2,1)}...) custom-call(bf16[2,8,3456]{2,1,0:T(8,128)(2,1)} %copy-done.24, ...), custom_call_target="tpu_custom_call" | custom-call | tf_op jit(solution)/shard_map/experts/pallas_call | solution.py:196
  370.5 34.9 %all_to_all.15 = bf16[8,384,384]{2,1,0:T(8,128)(2,1)} all-to-all(bf16[8,384,384]{2,1,0:T(8,128)(2,1)} %bitcast.28), channel_id=1, replica_groups=mesh['section'=4,'dp'=8,'expert'=32] {'dp'}, dimensions={0} | all-to-all | bytes 4718592 | tf_op jit(solution)/shard_map/all_to_all | solution.py:270
  412.9 17.4 %collective-permute-start.18 = (bf16[2,8,3584]{2,1,0:T(8,128)(2,1)S(1)}, bf16[2,8,3584]{2,1,0:T(8,128)(2,1)S(1)}, u32[]{:S(2)}, u32[]{:S(2)}) collective-permute-start(bf16[2,8,3584]{2,1,0:T(8,128)(2,1)S(1)} %copy-done.32), channel_id=1, source_target_pairs={{0,7},{1,8},{2,9},{3,10},{4,11},{5,12},{6,13},{7,14},{8,15},{9,16}... | collective-permute-start | bytes 344072 | tf_op jit(solution)/shard_map/ppermute | solution.py:18
  446.4 12.1 %collective-permute-start.32 = (bf16[1,8,3584]{2,1,0:T(8,128)(2,1)S(1)}, bf16[1,8,3584]{2,1,0:T(8,128)(2,1)S(1)}, u32[]{:S(2)}, u32[]{:S(2)}) collective-permute-start(bf16[1,8,3584]{2,1,0:T(8,128)(2,1)S(1)} %copy-done.33), channel_id=1, source_target_pairs={{0,24},{1,25},{2,26},{3,27},{4,28},{5,29},{6,30},{7,31},{8,0},{9,1... | collective-permute-start | bytes 172040 | tf_op jit(solution)/shard_map/ppermute | solution.py:18
  458.5 9.6 %collective-permute-done.32.refs_19_ = bf16[1,8,3584]{2,1,0:T(8,128)(2,1)S(1)} collective-permute-done((bf16[1,8,3584]{2,1,0:T(8,128)(2,1)S(1)}, bf16[1,8,3584]{2,1,0:T(8,128)(2,1)S(1)}, u32[]{:S(2)}, u32[]{:S(2)}) %collective-permute-start.32) | collective-permute-done | bytes 57376 | tf_op jit(solution)/shard_map/ppermute | solution.py:18
  519.5 8.7 %collective-permute-done.29.refs_16_ = bf16[2,8,3584]{2,1,0:T(8,128)(2,1)} collective-permute-done((bf16[2,8,3584]{2,1,0:T(8,128)(2,1)}, bf16[2,8,3584]{2,1,0:T(8,128)(2,1)}, u32[]{:S(2)}, u32[]{:S(2)}) %collective-permute-start.29) | collective-permute-done | bytes 114720 | tf_op jit(solution)/shard_map/ppermute | solution.py:18
  528.3 31.9 %collective-permute-done.30.refs_17_ = bf16[2,8,3584]{2,1,0:T(8,128)(2,1)} collective-permute-done((bf16[2,8,3584]{2,1,0:T(8,128)(2,1)}, bf16[2,8,3584]{2,1,0:T(8,128)(2,1)}, u32[]{:S(2)}, u32[]{:S(2)}) %collective-permute-start.30) | collective-permute-done | bytes 114720 | tf_op jit(solution)/shard_map/ppermute | solution.py:18
  571.2 10.5 %collective-permute-start.34 = (bf16[384,384]{1,0:T(8,128)(2,1)S(1)}, bf16[384,384]{1,0:T(8,128)(2,1)}, u32[]{:S(2)}, u32[]{:S(2)}) collective-permute-start(bf16[384,384]{1,0:T(8,128)(2,1)S(1)} %reduce_sum.22), channel_id=1, source_target_pairs={{0,16},{1,17},{2,18},{3,19},{4,20},{5,21},{6,22},{7,23},{8,24},{9,... | collective-permute-start | bytes 884744 | tf_op jit(solution)/shard_map/ppermute | solution.py:18
  586.1 53.7 %collective-permute-done.34 = bf16[384,384]{1,0:T(8,128)(2,1)} collective-permute-done((bf16[384,384]{1,0:T(8,128)(2,1)S(1)}, bf16[384,384]{1,0:T(8,128)(2,1)}, u32[]{:S(2)}, u32[]{:S(2)}) %collective-permute-start.34) | collective-permute-done | bytes 294944 | tf_op jit(solution)/shard_map/ppermute | solution.py:18
  (135 shorter events, 152.2 us)
Async XLA Ops:
  2.5 50.9 %collective-permute-start.16 = (bf16[3,384,128]{2,1,0:T(8,128)(2,1)S(1)}, bf16[3,384,128]{2,1,0:T(8,128)(2,1)S(1)}, u32[]{:S(2)}, u32[]{:S(2)}) collective-permute-start(bf16[3,384,128]{2,1,0:T(8,128)(2,1)S(1)} %pad_maximum_fusion), channel_id=1, source_target_pairs={{0,16},{1,17},{2,18},{3,19},{4,20},{5,21},{6,22},{7,23},{8,24},{9,... | collective-permute-start | bytes 884744 | tf_op jit(solution)/shard_map/ppermute | solution.py:18
  55.4 301.5 %all-to-all-start = ((bf16[8,3,384,128]{3,2,1,0:T(8,128)(2,1)}), bf16[8,3,384,128]{3,2,1,0:T(8,128)(2,1)S(1)}, u32[]{:S(2)}, u32[]{:S(2)}) async-start(bf16[8,3,384,128]{3,2,1,0:T(8,128)(2,1)} %broadcast_in_dim.15), calls=%async_computation | async-start | bytes 4718592 | tf_op jit(solution)/shard_map/all_to_all | solution.py:264
  66.4 67.7 %collective-permute-start = (bf16[2,8,3456]{2,1,0:T(8,128)(2,1)}, bf16[2,8,3456]{2,1,0:T(8,128)(2,1)S(1)}, u32[]{:S(2)}, u32[]{:S(2)}) collective-permute-start(bf16[2,8,3456]{2,1,0:T(8,128)(2,1)} %get-tuple-element.41), channel_id=1, source_target_pairs={{0,24},{1,25},{2,26},{3,27},{4,28},{5,29},{6,30},{7,31},{8,0},{9,1... | collective-permute-start | bytes 331784 | tf_op jit(solution)/shard_map/ppermute | solution.py:18
  97.5 60.9 %collective-permute-start.1 = (bf16[4,8,3456]{2,1,0:T(8,128)(2,1)}, bf16[4,8,3456]{2,1,0:T(8,128)(2,1)S(1)}, u32[]{:S(2)}, u32[]{:S(2)}) collective-permute-start(bf16[4,8,3456]{2,1,0:T(8,128)(2,1)} %get-tuple-element.42), channel_id=1, source_target_pairs={{0,25},{1,26},{2,27},{3,28},{4,29},{5,30},{6,31},{7,0},{8,1},{9,2}... | collective-permute-start | bytes 663560 | tf_op jit(solution)/shard_map/ppermute | solution.py:18
  105.6 70.6 %collective-permute-start.2 = (bf16[4,8,3456]{2,1,0:T(8,128)(2,1)}, bf16[4,8,3456]{2,1,0:T(8,128)(2,1)S(1)}, u32[]{:S(2)}, u32[]{:S(2)}) collective-permute-start(bf16[4,8,3456]{2,1,0:T(8,128)(2,1)} %get-tuple-element.43), channel_id=1, source_target_pairs={{0,26},{1,27},{2,28},{3,29},{4,30},{5,31},{6,0},{7,1},{8,2},{9,3},... | collective-permute-start | bytes 663560 | tf_op jit(solution)/shard_map/ppermute | solution.py:18
  108.7 86.7 %collective-permute-start.3 = (bf16[4,8,3456]{2,1,0:T(8,128)(2,1)}, bf16[4,8,3456]{2,1,0:T(8,128)(2,1)S(1)}, u32[]{:S(2)}, u32[]{:S(2)}) collective-permute-start(bf16[4,8,3456]{2,1,0:T(8,128)(2,1)} %get-tuple-element.44), channel_id=1, source_target_pairs={{0,27},{1,28},{2,29},{3,30},{4,31},{5,0},{6,1},{7,2},{8,3},{9,4},{... | collective-permute-start | bytes 663560 | tf_op jit(solution)/shard_map/ppermute | solution.py:18
  120.3 98.5 %collective-permute-start.4 = (bf16[4,8,3456]{2,1,0:T(8,128)(2,1)}, bf16[4,8,3456]{2,1,0:T(8,128)(2,1)S(1)}, u32[]{:S(2)}, u32[]{:S(2)}) collective-permute-start(bf16[4,8,3456]{2,1,0:T(8,128)(2,1)} %get-tuple-element.45), channel_id=1, source_target_pairs={{0,28},{1,29},{2,30},{3,31},{4,0},{5,1},{6,2},{7,3},{8,4},{9,5},{1... | collective-permute-start | bytes 663560 | tf_op jit(solution)/shard_map/ppermute | solution.py:18
  151.4 69.3 %collective-permute-start.5 = (bf16[4,8,3456]{2,1,0:T(8,128)(2,1)}, bf16[4,8,3456]{2,1,0:T(8,128)(2,1)S(1)}, u32[]{:S(2)}, u32[]{:S(2)}) collective-permute-start(bf16[4,8,3456]{2,1,0:T(8,128)(2,1)} %get-tuple-element.46), channel_id=1, source_target_pairs={{0,29},{1,30},{2,31},{3,0},{4,1},{5,2},{6,3},{7,4},{8,5},{9,6},{10... | collective-permute-start | bytes 663560 | tf_op jit(solution)/shard_map/ppermute | solution.py:18
  158.4 81.1 %collective-permute-start.6 = (bf16[4,8,3456]{2,1,0:T(8,128)(2,1)}, bf16[4,8,3456]{2,1,0:T(8,128)(2,1)S(1)}, u32[]{:S(2)}, u32[]{:S(2)}) collective-permute-start(bf16[4,8,3456]{2,1,0:T(8,128)(2,1)} %get-tuple-element.47), channel_id=1, source_target_pairs={{0,30},{1,31},{2,0},{3,1},{4,2},{5,3},{6,4},{7,5},{8,6},{9,7},{10,... | collective-permute-start | bytes 663560 | tf_op jit(solution)/shard_map/ppermute | solution.py:18
  176.2 69.3 %collective-permute-start.7 = (bf16[4,8,3456]{2,1,0:T(8,128)(2,1)}, bf16[4,8,3456]{2,1,0:T(8,128)(2,1)S(1)}, u32[]{:S(2)}, u32[]{:S(2)}) collective-permute-start(bf16[4,8,3456]{2,1,0:T(8,128)(2,1)} %get-tuple-element.48), channel_id=1, source_target_pairs={{0,31},{1,0},{2,1},{3,2},{4,3},{5,4},{6,5},{7,6},{8,7},{9,8},{10,9... | collective-permute-start | bytes 663560 | tf_op jit(solution)/shard_map/ppermute | solution.py:18
  195.5 52.0 %collective-permute-start.8 = (bf16[4,8,3456]{2,1,0:T(8,128)(2,1)}, bf16[4,8,3456]{2,1,0:T(8,128)(2,1)S(1)}, u32[]{:S(2)}, u32[]{:S(2)}) collective-permute-start(bf16[4,8,3456]{2,1,0:T(8,128)(2,1)} %get-tuple-element.50), channel_id=1, source_target_pairs={{0,1},{1,2},{2,3},{3,4},{4,5},{5,6},{6,7},{7,8},{8,9},{9,10},{10,1... | collective-permute-start | bytes 663560 | tf_op jit(solution)/shard_map/ppermute | solution.py:18
  218.8 41.2 %collective-permute-start.9 = (bf16[4,8,3456]{2,1,0:T(8,128)(2,1)}, bf16[4,8,3456]{2,1,0:T(8,128)(2,1)S(1)}, u32[]{:S(2)}, u32[]{:S(2)}) collective-permute-start(bf16[4,8,3456]{2,1,0:T(8,128)(2,1)} %get-tuple-element.51), channel_id=1, source_target_pairs={{0,2},{1,3},{2,4},{3,5},{4,6},{5,7},{6,8},{7,9},{8,10},{9,11},{10,... | collective-permute-start | bytes 663560 | tf_op jit(solution)/shard_map/ppermute | solution.py:18
  220.7 46.0 %collective-permute-start.10 = (bf16[4,8,3456]{2,1,0:T(8,128)(2,1)}, bf16[4,8,3456]{2,1,0:T(8,128)(2,1)S(1)}, u32[]{:S(2)}, u32[]{:S(2)}) collective-permute-start(bf16[4,8,3456]{2,1,0:T(8,128)(2,1)} %get-tuple-element.52), channel_id=1, source_target_pairs={{0,3},{1,4},{2,5},{3,6},{4,7},{5,8},{6,9},{7,10},{8,11},{9,12},{10... | collective-permute-start | bytes 663560 | tf_op jit(solution)/shard_map/ppermute | solution.py:18
  245.5 43.3 %collective-permute-start.12 = (bf16[4,8,3456]{2,1,0:T(8,128)(2,1)}, bf16[4,8,3456]{2,1,0:T(8,128)(2,1)S(1)}, u32[]{:S(2)}, u32[]{:S(2)}) collective-permute-start(bf16[4,8,3456]{2,1,0:T(8,128)(2,1)} %get-tuple-element.54), channel_id=1, source_target_pairs={{0,5},{1,6},{2,7},{3,8},{4,9},{5,10},{6,11},{7,12},{8,13},{9,14},{... | collective-permute-start | bytes 663560 | tf_op jit(solution)/shard_map/ppermute | solution.py:18
  247.4 72.6 %collective-permute-start.13 = (bf16[4,8,3456]{2,1,0:T(8,128)(2,1)}, bf16[4,8,3456]{2,1,0:T(8,128)(2,1)S(1)}, u32[]{:S(2)}, u32[]{:S(2)}) collective-permute-start(bf16[4,8,3456]{2,1,0:T(8,128)(2,1)} %get-tuple-element.55), channel_id=1, source_target_pairs={{0,6},{1,7},{2,8},{3,9},{4,10},{5,11},{6,12},{7,13},{8,14},{9,15},... | collective-permute-start | bytes 663560 | tf_op jit(solution)/shard_map/ppermute | solution.py:18
  260.0 96.8 %collective-permute-start.14 = (bf16[4,8,3456]{2,1,0:T(8,128)(2,1)}, bf16[4,8,3456]{2,1,0:T(8,128)(2,1)}, u32[]{:S(2)}, u32[]{:S(2)}) collective-permute-start(bf16[4,8,3456]{2,1,0:T(8,128)(2,1)} %get-tuple-element.56), channel_id=1, source_target_pairs={{0,7},{1,8},{2,9},{3,10},{4,11},{5,12},{6,13},{7,14},{8,15},{9,16}... | collective-permute-start | bytes 663560 | tf_op jit(solution)/shard_map/ppermute | solution.py:18
  405.4 180.4 %all-to-all-start.1 = ((bf16[8,384,384]{2,1,0:T(8,128)(2,1)}), bf16[8,384,384]{2,1,0:T(8,128)(2,1)S(1)}, u32[]{:S(2)}, u32[]{:S(2)}) async-start(bf16[8,384,384]{2,1,0:T(8,128)(2,1)} %bitcast.27), calls=%async_computation.1 | async-start | bytes 4718592 | tf_op jit(solution)/shard_map/all_to_all | solution.py:270
  412.9 57.1 %collective-permute-start.18 = (bf16[2,8,3584]{2,1,0:T(8,128)(2,1)S(1)}, bf16[2,8,3584]{2,1,0:T(8,128)(2,1)S(1)}, u32[]{:S(2)}, u32[]{:S(2)}) collective-permute-start(bf16[2,8,3584]{2,1,0:T(8,128)(2,1)S(1)} %copy-done.32), channel_id=1, source_target_pairs={{0,7},{1,8},{2,9},{3,10},{4,11},{5,12},{6,13},{7,14},{8,15},{9,16}... | collective-permute-start | bytes 344072 | tf_op jit(solution)/shard_map/ppermute | solution.py:18
  430.3 41.7 %collective-permute-start.19 = (bf16[2,8,3584]{2,1,0:T(8,128)(2,1)S(1)}, bf16[2,8,3584]{2,1,0:T(8,128)(2,1)S(1)}, u32[]{:S(2)}, u32[]{:S(2)}) collective-permute-start(bf16[2,8,3584]{2,1,0:T(8,128)(2,1)S(1)} %copy-done.31), channel_id=1, source_target_pairs={{0,6},{1,7},{2,8},{3,9},{4,10},{5,11},{6,12},{7,13},{8,14},{9,15},... | collective-permute-start | bytes 344072 | tf_op jit(solution)/shard_map/ppermute | solution.py:18
  436.3 44.9 %collective-permute-start.20 = (bf16[2,8,3584]{2,1,0:T(8,128)(2,1)S(1)}, bf16[2,8,3584]{2,1,0:T(8,128)(2,1)S(1)}, u32[]{:S(2)}, u32[]{:S(2)}) collective-permute-start(bf16[2,8,3584]{2,1,0:T(8,128)(2,1)S(1)} %copy-done.30), channel_id=1, source_target_pairs={{0,5},{1,6},{2,7},{3,8},{4,9},{5,10},{6,11},{7,12},{8,13},{9,14},{... | collective-permute-start | bytes 344072 | tf_op jit(solution)/shard_map/ppermute | solution.py:18
  438.2 49.5 %collective-permute-start.21 = (bf16[2,8,3584]{2,1,0:T(8,128)(2,1)S(1)}, bf16[2,8,3584]{2,1,0:T(8,128)(2,1)S(1)}, u32[]{:S(2)}, u32[]{:S(2)}) collective-permute-start(bf16[2,8,3584]{2,1,0:T(8,128)(2,1)S(1)} %copy-done.29), channel_id=1, source_target_pairs={{0,4},{1,5},{2,6},{3,7},{4,8},{5,9},{6,10},{7,11},{8,12},{9,13},{1... | collective-permute-start | bytes 344072 | tf_op jit(solution)/shard_map/ppermute | solution.py:18
  505.2 54.9 %collective-permute-start.30 = (bf16[2,8,3584]{2,1,0:T(8,128)(2,1)}, bf16[2,8,3584]{2,1,0:T(8,128)(2,1)}, u32[]{:S(2)}, u32[]{:S(2)}) collective-permute-start(bf16[2,8,3584]{2,1,0:T(8,128)(2,1)} %get-tuple-element.72), channel_id=1, source_target_pairs={{0,26},{1,27},{2,28},{3,29},{4,30},{5,31},{6,0},{7,1},{8,2},{9,3},... | collective-permute-start | bytes 344072 | tf_op jit(solution)/shard_map/ppermute | solution.py:18
  512.6 47.6 %collective-permute-start.31 = (bf16[2,8,3584]{2,1,0:T(8,128)(2,1)}, bf16[2,8,3584]{2,1,0:T(8,128)(2,1)}, u32[]{:S(2)}, u32[]{:S(2)}) collective-permute-start(bf16[2,8,3584]{2,1,0:T(8,128)(2,1)} %get-tuple-element.73), channel_id=1, source_target_pairs={{0,25},{1,26},{2,27},{3,28},{4,29},{5,30},{6,31},{7,0},{8,1},{9,2}... | collective-permute-start | bytes 344072 | tf_op jit(solution)/shard_map/ppermute | solution.py:18
  571.2 68.6 %collective-permute-start.34 = (bf16[384,384]{1,0:T(8,128)(2,1)S(1)}, bf16[384,384]{1,0:T(8,128)(2,1)}, u32[]{:S(2)}, u32[]{:S(2)}) collective-permute-start(bf16[384,384]{1,0:T(8,128)(2,1)S(1)} %reduce_sum.22), channel_id=1, source_target_pairs={{0,16},{1,17},{2,18},{3,19},{4,20},{5,21},{6,22},{7,23},{8,24},{9,... | collective-permute-start | bytes 884744 | tf_op jit(solution)/shard_map/ppermute | solution.py:18
  (49 other events, 2617.0 us)

commit v2 on v1

--- a/solution.py
+++ b/solution.py
@@ -13,21 +13,38 @@
 EXTRA = 128
 
 
+COPIES = 4
+
+
 def shifted(value, axis, steps):
     count = lax.axis_size(axis)
     return lax.ppermute(value, axis, [(s, (s + steps) % count) for s in range(count)])
 
 
+def sent_back(value, steps):
+    sections, count = lax.axis_size("section"), lax.axis_size("expert")
+    pairs = [
+        (s * count + e, (s - 1) % sections * count + (e + steps) % count)
+        for s in range(sections)
+        for e in range(count)
+    ]
+    return lax.ppermute(value, ("section", "expert"), pairs)
+
+
 def offsets_of(reach):
     return list(range(-reach, reach + 1))
 
 
+def hosts_of(d, reach):
+    return tuple(range(0, COPIES, 2)) if abs(d) == reach else tuple(range(COPIES))
+
+
 def blocks_of(d, reach):
-    return (d + reach,) if abs(d) == reach else (d + reach, d + 3 * reach)
+    return tuple((d + reach + 2 * reach * k) % (2 * reach * COPIES) for k in hosts_of(d, reach))
 
 
 def selectors(routes_ref, here, experts):
-    reach = experts // 4
+    reach = experts // (2 * COPIES)
     tokens = routes_ref.shape[1]
     ids = lax.broadcasted_iota(jnp.int32, (experts, tokens), 0)
     picks = [routes_ref[k : k + 1, :] for k in range(2)]
@@ -53,7 +70,7 @@
 
 
 def pack_kernel(here_ref, routes_ref, combine_ref, rows_ref, grads_ref, *outs, experts):
-    reach = experts // 4
+    reach = experts // (2 * COPIES)
     width = rows_ref.shape[1]
     fold = width // SUB
     main, ninth, sub = selectors(routes_ref, here_ref[0], experts)
@@ -81,7 +98,7 @@
 
 
 def pack(here, routes_t, combine_t, rows, grads, experts):
-    reach = experts // 4
+    reach = experts // (2 * COPIES)
     width = rows.shape[1]
     vmem = pl.BlockSpec(memory_space=pltpu.VMEM)
     shapes = [
@@ -98,10 +115,10 @@
     )(here, routes_t, combine_t, rows, grads)
 
 
-def gather_blocks(ref_of, count, scratch, folded, width, picks):
+def gather_blocks(blocks, scratch, folded, width, picks):
     fold = width // SUB
-    for b in range(count):
-        block = ref_of(b)
+    count = len(blocks)
+    for b, block in enumerate(blocks):
         scratch[b * SUB : (b + 1) * SUB, :] = block[:, 0:width]
         folded[b * SUB : (b + 1) * SUB, :] = block[:, width : width + fold]
     whole = folded[0 : count * SUB, :]
@@ -111,35 +128,38 @@
 
 
 def expert_kernel(*refs, experts):
-    reach = experts // 4
+    reach = experts // (2 * COPIES)
     offsets = offsets_of(reach)
     arrived = refs[: len(offsets)]
     own_w = refs[len(offsets) : len(offsets) + 3]
-    far_w = refs[len(offsets) + 3]
-    at = len(offsets) + 4
+    side_w, far_w = refs[len(offsets) + 3 : len(offsets) + 5]
+    at = len(offsets) + 5
     returned = refs[at : at + len(offsets)]
-    terms = refs[at + len(offsets) : at + len(offsets) + 2]
-    x_ref, g_ref, folded = refs[at + len(offsets) + 2 :]
+    own_t, side_t, far_t = refs[at + len(offsets) : at + len(offsets) + 3]
+    x_ref, g_ref, folded = refs[at + len(offsets) + 3 :]
     width = own_w[0].shape[0]
     ff = own_w[0].shape[1]
     fold = width // SUB
     by_hidden = (((1,), (1,)), ((), ()))
     by_rows = (((0,), (0,)), ((), ()))
-    for half in range(2):
-        reached = reach if half == 0 else reach - 1
-        here = [(d, arrived[d + reach]) for d in range(-reached, reached + 1)]
+    for k in range(COPIES):
+        here = [(d, hosts_of(d, reach).index(k)) for d in offsets if k in hosts_of(d, reach)]
         count = len(here)
         padded = -(-count // SUB) * SUB
         rows = count * SUB + padded
         r0 = lax.broadcasted_iota(jnp.int32, (padded, count * SUB), 0)
         r1 = lax.broadcasted_iota(jnp.int32, (padded, count * SUB), 1)
         picks = [jnp.where(r1 == r0 * SUB + s, 1.0, 0.0).astype(BF16) for s in range(SUB)]
-        gather_blocks(lambda b: here[b][1].at[2 * half], count, x_ref, folded, width, picks)
-        gather_blocks(lambda b: here[b][1].at[2 * half + 1], count, g_ref, folded, width, picks)
-        if half == 0:
+        blocks = [arrived[d + reach].at[2 * i] for d, i in here]
+        gather_blocks(blocks, x_ref, folded, width, picks)
+        blocks = [arrived[d + reach].at[2 * i + 1] for d, i in here]
+        gather_blocks(blocks, g_ref, folded, width, picks)
+        if k == 0:
             gate_w, up_w, down_w = [w[...] for w in own_w]
+        elif k == 2:
+            gate_w, up_w, down_w = [far_w[:, i].reshape(width, ff) for i in range(3)]
         else:
-            gate_w, up_w, down_w = [far_w[:, i].reshape(width, ff) for i in range(3)]
+            gate_w, up_w, down_w = [side_w[:, k // 2, i].reshape(width, ff) for i in range(3)]
         x = x_ref[0:rows, :]
         g = g_ref[0:rows, :]
         gate = jnp.dot(x, gate_w, preferred_element_type=F32)
@@ -166,37 +186,42 @@
         nine_sum = jnp.dot(spread[0], nine_sum, preferred_element_type=F32)
         lane = lax.broadcasted_iota(jnp.int32, (count * SUB, EXTRA), 1)
         extra = jnp.where(lane == 0, weighed[0 : count * SUB, :], jnp.where(lane == 1, nine_sum, 0.0))
-        for b, (d, _) in enumerate(here):
+        for b, (d, i) in enumerate(here):
             out = returned[d + reach]
             span = slice(b * SUB, (b + 1) * SUB)
-            out[half, :, 0:width] = slot_grad[span, :].astype(BF16)
-            out[half, :, width : width + fold] = tail[span, :].astype(BF16)
-            out[half, :, width + fold : width + fold + EXTRA] = extra[span, :].astype(BF16)
-        term = terms[half]
-        term[:, 0:ff] = lax.dot_general(x, d_gate, by_rows, preferred_element_type=F32).astype(BF16)
-        term[:, ff : 2 * ff] = lax.dot_general(x, d_up, by_rows, preferred_element_type=F32).astype(
-            BF16
-        )
-        term[:, 2 * ff : 3 * ff] = lax.dot_general(
-            g, hidden, by_rows, preferred_element_type=F32
-        ).astype(BF16)
-
-
-def run_experts(arrived, own_w, far_w, experts):
-    reach = experts // 4
+            out[i, :, 0:width] = slot_grad[span, :].astype(BF16)
+            out[i, :, width : width + fold] = tail[span, :].astype(BF16)
+            out[i, :, width + fold : width + fold + EXTRA] = extra[span, :].astype(BF16)
+        for i, (left, right) in enumerate(((x, d_gate), (x, d_up), (g, hidden))):
+            cols = slice(i * ff, (i + 1) * ff)
+            term = lax.dot_general(left, right, by_rows, preferred_element_type=F32).astype(BF16)
+            if k == 0:
+                own_t[:, :, cols] = term.reshape(own_t.shape[0], -1, ff)
+            elif k == 2:
+                far_t[:, :, cols] = term.reshape(far_t.shape[0], -1, ff)
+            else:
+                side_t[:, k // 2, :, cols] = term.reshape(side_t.shape[0], -1, ff)
+
+
+def run_experts(arrived, own_w, side_w, far_w, experts):
+    reach = experts // (2 * COPIES)
     width, ff = own_w[0].shape
     fold = width // SUB
+    replicas = far_w.shape[0]
     vmem = pl.BlockSpec(memory_space=pltpu.VMEM)
     shapes = [
         jax.ShapeDtypeStruct((len(blocks_of(d, reach)), SUB, width + fold + EXTRA), BF16)
         for d in offsets_of(reach)
-    ] + [jax.ShapeDtypeStruct((width, 3 * ff), BF16)] * 2
+    ] + [
+        jax.ShapeDtypeStruct((replicas,) + lead + (width // replicas, 3 * ff), BF16)
+        for lead in ((), (2,), ())
+    ]
     count = 2 * reach + 1
     rows = count * SUB + -(-count // SUB) * SUB
     outs = pl.pallas_call(
         lambda *refs: expert_kernel(*refs, experts=experts),
         out_shape=shapes,
-        in_specs=[vmem] * (len(arrived) + 4),
+        in_specs=[vmem] * (len(arrived) + 5),
         out_specs=[vmem] * len(shapes),
         scratch_shapes=[
             pltpu.VMEM((rows, width), BF16),
@@ -205,23 +230,35 @@
         ],
         name="experts",
         interpret=INTERPRET,
-    )(*arrived, *own_w, far_w)
-    return outs[:-2], outs[-2], outs[-1]
-
-
-def unpack_kernel(here_ref, routes_ref, combine_ref, *refs, experts):
-    reach = experts // 4
+    )(*arrived, *own_w, side_w, far_w)
+    return outs[:-3], outs[-3:]
+
+
+def scalars_kernel(here_ref, routes_ref, combine_ref, *refs, experts):
+    reach = experts // (2 * COPIES)
     offsets = offsets_of(reach)
-    arrived = refs[: len(offsets)]
-    grad_out, combine_out, body, tail, extra = refs[len(offsets) :]
+    combine_out, extra = refs[len(offsets) :]
+    for d, ref in zip(offsets, refs):
+        for i, b in enumerate(blocks_of(d, reach)):
+            extra[b * SUB : (b + 1) * SUB, :] = ref[i].astype(F32)
+    main, ninth, sub = selectors(routes_ref, here_ref[0], experts)
+    for k in range(2):
+        value = main[k] * extra[:, 0:1] + jnp.where(sub == 0, ninth[k], 0.0) * extra[:, 1:2]
+        value = jnp.sum(value, axis=0, keepdims=True)
+        combine_out[k : k + 1, :] = value / combine_ref[k : k + 1, :]
+
+
+def unpack_kernel(here_ref, routes_ref, *refs, experts):
+    reach = experts // (2 * COPIES)
+    offsets = offsets_of(reach)
+    grad_out, body, tail = refs[len(offsets) :]
     width = body.shape[1]
     fold = tail.shape[1]
-    for d, ref in zip(offsets, arrived):
+    for d, ref in zip(offsets, refs):
         for i, b in enumerate(blocks_of(d, reach)):
             span = slice(b * SUB, (b + 1) * SUB)
             body[span, :] = ref[i, :, 0:width]
             tail[span, :] = ref[i, :, width : width + fold]
-            extra[span, :] = ref[i, :, width + fold : width + fold + EXTRA].astype(F32)
     main, ninth, sub = selectors(routes_ref, here_ref[0], experts)
     pick = (main[0] + main[1]).T.astype(BF16)
     nine = ninth[0] + ninth[1]
@@ -232,31 +269,38 @@
             jnp.where(sub == s, nine, 0.0).T.astype(BF16), tail[...], preferred_element_type=F32
         )
         grad_out[:, cols] = total.astype(BF16)
-    for k in range(2):
-        value = main[k] * extra[:, 0:1] + jnp.where(sub == 0, ninth[k], 0.0) * extra[:, 1:2]
-        value = jnp.sum(value, axis=0, keepdims=True)
-        combine_out[k : k + 1, :] = value / combine_ref[k : k + 1, :].astype(F32)
-
-
-def unpack(here, routes_t, combine_t, arrived, width, experts):
-    tokens = routes_t.shape[1]
+
+
+def unpack_scalars(here, routes_t, combine_t, arrived, width, experts):
+    vmem = pl.BlockSpec(memory_space=pltpu.VMEM)
+    at = (width + width // SUB) // EXTRA
+    lanes = [pl.BlockSpec((a.shape[0], SUB, EXTRA), lambda i: (0, 0, at)) for a in arrived]
+    return pl.pallas_call(
+        lambda *refs: scalars_kernel(*refs, experts=experts),
+        grid=(1,),
+        out_shape=jax.ShapeDtypeStruct(routes_t.shape, F32),
+        in_specs=[pl.BlockSpec(memory_space=pltpu.SMEM), vmem, vmem] + lanes,
+        out_specs=vmem,
+        scratch_shapes=[pltpu.VMEM((experts * SUB, EXTRA), F32)],
+        name="scalars",
+        interpret=INTERPRET,
+    )(here, routes_t, combine_t, *arrived)
+
+
+def unpack(here, routes_t, arrived, width, experts):
     vmem = pl.BlockSpec(memory_space=pltpu.VMEM)
     return pl.pallas_call(
         lambda *refs: unpack_kernel(*refs, experts=experts),
-        out_shape=[
-            jax.ShapeDtypeStruct((tokens, width), BF16),
-            jax.ShapeDtypeStruct((2, tokens), F32),
-        ],
-        in_specs=[pl.BlockSpec(memory_space=pltpu.SMEM)] + [vmem] * (2 + len(arrived)),
-        out_specs=[vmem] * 2,
+        out_shape=jax.ShapeDtypeStruct((routes_t.shape[1], width), BF16),
+        in_specs=[pl.BlockSpec(memory_space=pltpu.SMEM)] + [vmem] * (1 + len(arrived)),
+        out_specs=vmem,
         scratch_shapes=[
             pltpu.VMEM((experts * SUB, width), BF16),
             pltpu.VMEM((experts * SUB, width // SUB), BF16),
-            pltpu.VMEM((experts * SUB, EXTRA), F32),
         ],
         name="unpack",
         interpret=INTERPRET,
-    )(here, routes_t, combine_t, *arrived)
+    )(here, routes_t, *arrived)
 
 
 def spread_over(x, axis):
@@ -264,9 +308,7 @@
     return lax.all_to_all(copies, axis, split_axis=0, concat_axis=0, tiled=True)
 
 
-def summed_on_arrival(term, axis):
-    count = lax.axis_size(axis)
-    pieces = term.reshape(count, term.shape[0] // count, term.shape[1])
+def summed_on_arrival(pieces, axis):
     arrived = lax.all_to_all(pieces, axis, split_axis=0, concat_axis=0, tiled=True)
     return arrived.astype(F32).sum(axis=0)
 
@@ -274,9 +316,11 @@
 def per_device(tokens_in, upstream, routes, combine, gate_proj, up_proj, down_proj):
     experts = lax.axis_size("expert")
     replicas = lax.axis_size("dp")
-    reach = experts // 4
+    reach = experts // (2 * COPIES)
+    period = 2 * reach
     width = tokens_in.shape[2]
-    assert 9 * tokens_in.shape[1] == 4 * experts * (SUB + 1)
+    tokens = tokens_in.shape[1]
+    assert 9 * tokens == 4 * experts * (SUB + 1)
     here = lax.axis_index("expert").astype(jnp.int32).reshape(1)
     routes_t = routes[0].T
     combine_t = combine[0].T
@@ -285,25 +329,37 @@
     start = lax.axis_index("dp") * part
     offsets = offsets_of(reach)
     piece = jnp.stack([lax.dynamic_slice_in_dim(w, start, part, 0) for w in own_w])
-    piece = shifted(piece, "expert", 2 * reach)
-    far_w = spread_over(piece, "dp")
+    side1 = shifted(piece, "expert", -period)
+    side3 = shifted(piece, "expert", period)
+    low = shifted(side1[:, : part // 2], "expert", -period)
+    high = shifted(side3[:, part // 2 :], "expert", period)
+    side_w = spread_over(jnp.stack([side1, side3]), "dp")
+    far_w = spread_over(jnp.concatenate([low, high], axis=1), "dp")
     packed = pack(here, routes_t, combine_t, tokens_in[0], upstream[0], experts)
+    behind = shifted(jnp.concatenate([routes_t.astype(F32), combine_t.astype(F32)]), "section", -1)
     arrived = list(packed)
     for i, d in enumerate(offsets):
         if d:
             arrived[i] = shifted(packed[i], "expert", d)
-    done, own_term, far_term = run_experts(arrived, own_w, far_w, experts)
-    back = list(done)
+    done, (own_t, side_t, far_t) = run_experts(arrived, own_w, side_w, far_w, experts)
+    back = []
     for i, d in enumerate(offsets):
-        if d:
-            back[i] = shifted(done[i], "expert", -d)
-    far_sum = summed_on_arrival(far_term, "dp").astype(BF16)
-    far_sum = shifted(far_sum, "expert", 2 * reach)
-    own_sum = summed_on_arrival(own_term, "dp")
-    weight_grad = (own_sum + far_sum.astype(F32)) * (1.0 / replicas)
-    token_grad, combine_grad = unpack(here, routes_t, combine_t, back, width, experts)
-    prev_grad = shifted(token_grad[None], "section", -1)
-    return prev_grad, weight_grad[None, None], combine_grad.astype(BF16).T[None]
+        back.append(sent_back(done[i], -d))
+    far_sum = summed_on_arrival(far_t, "dp").astype(BF16)
+    low = shifted(far_sum[: part // 2], "expert", period)
+    high = shifted(far_sum[part // 2 :], "expert", -period)
+    side_sum = summed_on_arrival(side_t, "dp")
+    joined = jnp.concatenate([side_sum[0, : part // 2] + low.astype(F32), side_sum[0, part // 2 :]])
+    side1 = shifted(joined.astype(BF16), "expert", period)
+    joined = jnp.concatenate([side_sum[1, : part // 2], side_sum[1, part // 2 :] + high.astype(F32)])
+    side3 = shifted(joined.astype(BF16), "expert", -period)
+    own_sum = summed_on_arrival(own_t, "dp")
+    weight_grad = (own_sum + side1.astype(F32) + side3.astype(F32)) * (1.0 / replicas)
+    routes_b = behind[:2].astype(jnp.int32)
+    combine_grad = unpack_scalars(here, routes_b, behind[2:], back, width, experts)
+    combine_grad = shifted(combine_grad, "section", 1)
+    prev_grad = unpack(here, routes_b, back, width, experts)
+    return prev_grad[None], weight_grad[None, None], combine_grad.astype(BF16).T[None]
 
 
 def solution(mesh):

time: 644 us -> 599 us (0.930)
  the two profiles are of different devices: /device:TPU:147 before, /device:TPU:104 now
where the time goes in v2:
time: 599 us; the launch traced here: 598 us
  waiting for transfers between devices  268 us (45%)
  starting transfers between devices  189 us (32%)
  blocking collectives  93.2 us (16%)
  Pallas kernels  26.8 us (4%)
  other arithmetic  10.5 us (2%)
  local copies, waits for them, and re-layouts  8.48 us (1%)
    ppermute x18, waiting for transfers between devices, shifted(): lax.ppermute(value, axis, [(s, (s + steps) % count) for s in range(count)])  225 us
    ppermute x18, starting transfers between devices, shifted(): lax.ppermute(value, axis, [(s, (s + steps) % count) for s in range(count)])  116 us
    all_to_all x2, blocking collectives, summed_on_arrival(): lax.all_to_all(pieces, axis, split_axis=0, concat_axis=0, tiled=True)  93.2 us
    ppermute x9, starting transfers between devices, sent_back(): return lax.ppermute(value, ('section', 'expert'), pairs)  60.9 us
    all_to_all x2, waiting for transfers between devices, spread_over(): return lax.all_to_all(copies, axis, split_axis=0, concat_axis=0, tiled=True)  29.9 us
    pallas_call x1, Pallas kernels, run_experts(): pl.pallas_call(lambda *refs: expert_kernel(*refs, experts=experts), out_s...  16.6 us
    ppermute x9, waiting for transfers between devices, sent_back(): return lax.ppermute(value, ('section', 'expert'), pairs)  13.7 us
  transfers between devices with their start and end apart: 30, of which 15 were waited for; matrix products, arithmetic and copies ran while one was open for 1% of the time, Pallas kernels for 2%

profile of v2, /device:TPU:104, one launch (start us, length us, event | category | flops | bytes accessed | tf_op | source)
XLA Modules:
  0.0 597.9 jit_solution(5548537317068615902)
XLA Ops:
  2.5 20.3 %collective-permute-start.9 = (bf16[3,384,128]{2,1,0:T(8,128)(2,1)S(1)}, bf16[3,384,128]{2,1,0:T(8,128)(2,1)S(1)}, u32[]{:S(2)}, u32[]{:S(2)}) collective-permute-start(bf16[3,384,128]{2,1,0:T(8,128)(2,1)S(1)} %pad_maximum_fusion.1), channel_id=1, source_target_pairs={{0,24},{1,25},{2,26},{3,27},{4,28},{5,29},{6,30},{7,31},{8,0},{9,1... | collective-permute-start | bytes 884744 | tf_op jit(solution)/shard_map/ppermute | solution.py:21
  24.8 49.4 %collective-permute-done.9 = bf16[3,384,128]{2,1,0:T(8,128)(2,1)S(1)} collective-permute-done((bf16[3,384,128]{2,1,0:T(8,128)(2,1)S(1)}, bf16[3,384,128]{2,1,0:T(8,128)(2,1)S(1)}, u32[]{:S(2)}, u32[]{:S(2)}) %collective-permute-start.9) | collective-permute-done | bytes 294944 | tf_op jit(solution)/shard_map/ppermute | solution.py:21
  74.2 13.2 %collective-permute-start.11 = (bf16[3,192,128]{2,1,0:T(8,128)(2,1)S(1)}, bf16[3,192,128]{2,1,0:T(8,128)(2,1)S(1)}, u32[]{:S(2)}, u32[]{:S(2)}) collective-permute-start(bf16[3,192,128]{2,1,0:T(8,128)(2,1)S(1)} %slice.42), channel_id=1, source_target_pairs={{0,24},{1,25},{2,26},{3,27},{4,28},{5,29},{6,30},{7,31},{8,0},{9,1... | collective-permute-start | bytes 442376 | tf_op jit(solution)/shard_map/ppermute | solution.py:21
  89.4 7.9 %collective-permute-done.11 = bf16[3,192,128]{2,1,0:T(8,128)(2,1)S(1)} collective-permute-done((bf16[3,192,128]{2,1,0:T(8,128)(2,1)S(1)}, bf16[3,192,128]{2,1,0:T(8,128)(2,1)S(1)}, u32[]{:S(2)}, u32[]{:S(2)}) %collective-permute-start.11) | collective-permute-done | bytes 147488 | tf_op jit(solution)/shard_map/ppermute | solution.py:21
  97.3 21.7 %collective-permute-done.12 = bf16[3,192,128]{2,1,0:T(8,128)(2,1)S(1)} collective-permute-done((bf16[3,192,128]{2,1,0:T(8,128)(2,1)S(1)}, bf16[3,192,128]{2,1,0:T(8,128)(2,1)S(1)}, u32[]{:S(2)}, u32[]{:S(2)}) %collective-permute-start.12) | collective-permute-done | bytes 147488 | tf_op jit(solution)/shard_map/ppermute | solution.py:21
  125.2 29.9 %all-to-all-done.1.refs_13_ = bf16[8,3,384,128]{3,2,1,0:T(8,128)(2,1)S(1)} async-done(((bf16[8,3,384,128]{3,2,1,0:T(8,128)(2,1)}), bf16[8,3,384,128]{3,2,1,0:T(8,128)(2,1)S(1)}, u32[]{:S(2)}, u32[]{:S(2)}) %all-to-all-start.1) | async-done | bytes 2359328 | tf_op jit(solution)/shard_map/all_to_all | solution.py:308
  172.0 7.9 %collective-permute-start.8 = (bf16[4,8,3456]{2,1,0:T(8,128)(2,1)}, bf16[4,8,3456]{2,1,0:T(8,128)(2,1)S(1)}, u32[]{:S(2)}, u32[]{:S(2)}) collective-permute-start(bf16[4,8,3456]{2,1,0:T(8,128)(2,1)} %get-tuple-element.32), channel_id=1, source_target_pairs={{0,4},{1,5},{2,6},{3,7},{4,8},{5,9},{6,10},{7,11},{8,12},{9,13},{1... | collective-permute-start | bytes 663560 | tf_op jit(solution)/shard_map/ppermute | solution.py:21
  184.6 29.0 %collective-permute-done.1.refs_0_ = bf16[4,8,3456]{2,1,0:T(8,128)(2,1)S(1)} collective-permute-done((bf16[4,8,3456]{2,1,0:T(8,128)(2,1)}, bf16[4,8,3456]{2,1,0:T(8,128)(2,1)S(1)}, u32[]{:S(2)}, u32[]{:S(2)}) %collective-permute-start.1) | collective-permute-done | bytes 221216 | tf_op jit(solution)/shard_map/ppermute | solution.py:21
  213.6 24.4 %collective-permute-start.5 = (bf16[8,8,3456]{2,1,0:T(8,128)(2,1)}, bf16[8,8,3456]{2,1,0:T(8,128)(2,1)S(1)}, u32[]{:S(2)}, u32[]{:S(2)}) collective-permute-start(bf16[8,8,3456]{2,1,0:T(8,128)(2,1)} %get-tuple-element.29), channel_id=1, source_target_pairs={{0,1},{1,2},{2,3},{3,4},{4,5},{5,6},{6,7},{7,8},{8,9},{9,10},{10,1... | collective-permute-start | bytes 1327112 | tf_op jit(solution)/shard_map/ppermute | solution.py:21
  242.1 8.1 %collective-permute-done.4.refs_3_ = bf16[8,8,3456]{2,1,0:T(8,128)(2,1)S(1)} collective-permute-done((bf16[8,8,3456]{2,1,0:T(8,128)(2,1)}, bf16[8,8,3456]{2,1,0:T(8,128)(2,1)S(1)}, u32[]{:S(2)}, u32[]{:S(2)}) %collective-permute-start.4) | collective-permute-done | bytes 442400 | tf_op jit(solution)/shard_map/ppermute | solution.py:21
  250.2 9.1 %collective-permute-done.5.refs_5_ = bf16[8,8,3456]{2,1,0:T(8,128)(2,1)S(1)} collective-permute-done((bf16[8,8,3456]{2,1,0:T(8,128)(2,1)}, bf16[8,8,3456]{2,1,0:T(8,128)(2,1)S(1)}, u32[]{:S(2)}, u32[]{:S(2)}) %collective-permute-start.5) | collective-permute-done | bytes 442400 | tf_op jit(solution)/shard_map/ppermute | solution.py:21
  259.3 18.3 %collective-permute-done.6.refs_6_ = bf16[8,8,3456]{2,1,0:T(8,128)(2,1)S(1)} collective-permute-done((bf16[8,8,3456]{2,1,0:T(8,128)(2,1)}, bf16[8,8,3456]{2,1,0:T(8,128)(2,1)S(1)}, u32[]{:S(2)}, u32[]{:S(2)}) %collective-permute-start.6) | collective-permute-done | bytes 442400 | tf_op jit(solution)/shard_map/ppermute | solution.py:21
  277.6 16.5 %collective-permute-done.7.refs_7_ = bf16[8,8,3456]{2,1,0:T(8,128)(2,1)S(1)} collective-permute-done((bf16[8,8,3456]{2,1,0:T(8,128)(2,1)}, bf16[8,8,3456]{2,1,0:T(8,128)(2,1)S(1)}, u32[]{:S(2)}, u32[]{:S(2)}) %collective-permute-start.7) | collective-permute-done | bytes 442400 | tf_op jit(solution)/shard_map/ppermute | solution.py:21
  294.9 16.6 %experts.1 = (bf16[2,8,3584]{2,1,0:T(8,128)(2,1)}, bf16[4,8,3584]{2,1,0:T(8,128)(2,1)}, bf16[4,8,3584]{2,1,0:T(8,128)(2,1)}, bf16[4,8,3584]{2,1,0:T(8,128)(2,1)}...) custom-call(bf16[4,8,3456]{2,1,0:T(8,128)(2,1)} %copy-done.14, ...), custom_call_target="tpu_custom_call" | custom-call | tf_op jit(solution)/shard_map/experts/pallas_call | solution.py:221
  311.5 34.6 %all_to_all.25 = bf16[8,384,384]{2,1,0:T(8,128)(2,1)} all-to-all(bf16[8,384,384]{2,1,0:T(8,128)(2,1)} %get-tuple-element.44), channel_id=1, replica_groups=mesh['section'=4,'dp'=8,'expert'=32] {'dp'}, dimensions={0} | all-to-all | bytes 4718592 | tf_op jit(solution)/shard_map/all_to_all | solution.py:312
  346.2 58.6 %all_to_all.26 = bf16[8,2,384,384]{3,2,1,0:T(8,128)(2,1)} all-to-all(bf16[8,2,384,384]{3,2,1,0:T(8,128)(2,1)S(1)} %copy-done.1), channel_id=1, replica_groups=mesh['section'=4,'dp'=8,'expert'=32] {'dp'}, dimensions={0} | all-to-all | bytes 9437184 | tf_op jit(solution)/shard_map/all_to_all | solution.py:312
  410.9 9.8 %collective-permute-start.14 = (bf16[4,8,3584]{2,1,0:T(8,128)(2,1)}, bf16[4,8,3584]{2,1,0:T(8,128)(2,1)S(1)}, u32[]{:S(2)}, u32[]{:S(2)}) collective-permute-start(bf16[4,8,3584]{2,1,0:T(8,128)(2,1)} %get-tuple-element.34), channel_id=1, source_target_pairs={{0,771},{1,772},{2,773},{3,774},{4,775},{5,776},{6,777},{7,778},{8... | collective-permute-start | bytes 688136 | tf_op jit(solution)/shard_map/ppermute | solution.py:31
  426.9 12.6 %collective-permute-start.24 = (bf16[192,384]{1,0:T(8,128)(2,1)S(1)}, bf16[192,384]{1,0:T(8,128)(2,1)S(1)}, u32[]{:S(2)}, u32[]{:S(2)}) collective-permute-start(bf16[192,384]{1,0:T(8,128)(2,1)S(1)} %get-tuple-element.50), channel_id=1, source_target_pairs={{0,24},{1,25},{2,26},{3,27},{4,28},{5,29},{6,30},{7,31},{8,0},{9,1... | collective-permute-start | bytes 442376 | tf_op jit(solution)/shard_map/ppermute | solution.py:21
  442.8 8.0 %collective-permute-done.22 = bf16[192,384]{1,0:T(8,128)(2,1)S(1)} collective-permute-done((bf16[192,384]{1,0:T(8,128)(2,1)S(1)}, bf16[192,384]{1,0:T(8,128)(2,1)S(1)}, u32[]{:S(2)}, u32[]{:S(2)}) %collective-permute-start.22) | collective-permute-done | bytes 147488 | tf_op jit(solution)/shard_map/ppermute | solution.py:21
  450.7 24.9 %collective-permute-start.16 = (bf16[4,8,3584]{2,1,0:T(8,128)(2,1)S(1)}, bf16[4,8,3584]{2,1,0:T(8,128)(2,1)S(1)}, u32[]{:S(2)}, u32[]{:S(2)}) collective-permute-start(bf16[4,8,3584]{2,1,0:T(8,128)(2,1)S(1)} %copy-done.22), channel_id=1, source_target_pairs={{0,769},{1,770},{2,771},{3,772},{4,773},{5,774},{6,775},{7,776},{8... | collective-permute-start | bytes 688136 | tf_op jit(solution)/shard_map/ppermute | solution.py:31
  481.0 8.4 %collective-permute-done.13.refs_2_.refs_3_ = bf16[2,8,3584]{2,1,0:T(8,128)(2,1)S(1)} collective-permute-done((bf16[2,8,3584]{2,1,0:T(8,128)(2,1)S(1)}, bf16[2,8,3584]{2,1,0:T(8,128)(2,1)S(1)}, u32[]{:S(2)}, u32[]{:S(2)}) %collective-permute-start.13) | collective-permute-done | bytes 114720 | tf_op jit(solution)/shard_map/ppermute | solution.py:31
  515.4 10.6 %collective-permute-start.23 = (bf16[384,384]{1,0:T(8,128)(2,1)}, bf16[384,384]{1,0:T(8,128)(2,1)}, u32[]{:S(2)}, u32[]{:S(2)}) collective-permute-start(bf16[384,384]{1,0:T(8,128)(2,1)} %pad_maximum_fusion.3), channel_id=1, source_target_pairs={{0,8},{1,9},{2,10},{3,11},{4,12},{5,13},{6,14},{7,15},{8,16},{9,17... | collective-permute-start | bytes 884744 | tf_op jit(solution)/shard_map/ppermute | solution.py:21
  538.2 11.4 %collective-permute-done.26 = bf16[2,128]{1,0:T(2,128)(2,1)S(1)} collective-permute-done((bf16[2,128]{1,0:T(2,128)(2,1)S(1)}, bf16[2,128]{1,0:T(2,128)(2,1)S(1)}, u32[]{:S(2)}, u32[]{:S(2)}) %collective-permute-start.26) | collective-permute-done | bytes 544 | tf_op jit(solution)/shard_map/ppermute | solution.py:21
  550.5 44.9 %collective-permute-done.25 = bf16[384,384]{1,0:T(8,128)(2,1)} collective-permute-done((bf16[384,384]{1,0:T(8,128)(2,1)}, bf16[384,384]{1,0:T(8,128)(2,1)}, u32[]{:S(2)}, u32[]{:S(2)}) %collective-permute-start.25) | collective-permute-done | bytes 294944 | tf_op jit(solution)/shard_map/ppermute | solution.py:21
  (117 shorter events, 100.6 us)
Async XLA Ops:
  2.5 71.6 %collective-permute-start.9 = (bf16[3,384,128]{2,1,0:T(8,128)(2,1)S(1)}, bf16[3,384,128]{2,1,0:T(8,128)(2,1)S(1)}, u32[]{:S(2)}, u32[]{:S(2)}) collective-permute-start(bf16[3,384,128]{2,1,0:T(8,128)(2,1)S(1)} %pad_maximum_fusion.1), channel_id=1, source_target_pairs={{0,24},{1,25},{2,26},{3,27},{4,28},{5,29},{6,30},{7,31},{8,0},{9,1... | collective-permute-start | bytes 884744 | tf_op jit(solution)/shard_map/ppermute | solution.py:21
  22.9 64.6 %collective-permute-start.10 = (bf16[3,384,128]{2,1,0:T(8,128)(2,1)S(1)}, bf16[3,384,128]{2,1,0:T(8,128)(2,1)S(1)}, u32[]{:S(2)}, u32[]{:S(2)}) collective-permute-start(bf16[3,384,128]{2,1,0:T(8,128)(2,1)S(1)} %pad_maximum_fusion.1), channel_id=1, source_target_pairs={{0,8},{1,9},{2,10},{3,11},{4,12},{5,13},{6,14},{7,15},{8,16},{9,17... | collective-permute-start | bytes 884744 | tf_op jit(solution)/shard_map/ppermute | solution.py:21
  87.4 31.5 %collective-permute-start.12 = (bf16[3,192,128]{2,1,0:T(8,128)(2,1)S(1)}, bf16[3,192,128]{2,1,0:T(8,128)(2,1)S(1)}, u32[]{:S(2)}, u32[]{:S(2)}) collective-permute-start(bf16[3,192,128]{2,1,0:T(8,128)(2,1)S(1)} %slice.43), channel_id=1, source_target_pairs={{0,8},{1,9},{2,10},{3,11},{4,12},{5,13},{6,14},{7,15},{8,16},{9,17... | collective-permute-start | bytes 442376 | tf_op jit(solution)/shard_map/ppermute | solution.py:21
  120.9 34.3 %all-to-all-start.1 = ((bf16[8,3,384,128]{3,2,1,0:T(8,128)(2,1)}), bf16[8,3,384,128]{3,2,1,0:T(8,128)(2,1)S(1)}, u32[]{:S(2)}, u32[]{:S(2)}) async-start(bf16[8,3,384,128]{3,2,1,0:T(8,128)(2,1)} %broadcast_in_dim.22), calls=%async_computation.1 | async-start | bytes 4718592 | tf_op jit(solution)/shard_map/all_to_all | solution.py:308
  158.4 135.7 %all-to-all-start = ((bf16[8,2,3,384,128]{4,3,2,1,0:T(8,128)(2,1)}), bf16[8,2,3,384,128]{4,3,2,1,0:T(8,128)(2,1)}, u32[]{:S(2)}, u32[]{:S(2)}) async-start(bf16[8,2,3,384,128]{4,3,2,1,0:T(8,128)(2,1)} %broadcast_in_dim.10), calls=%async_computation | async-start | bytes 9437184 | tf_op jit(solution)/shard_map/all_to_all | solution.py:308
  168.2 71.7 %collective-permute-start.2 = (bf16[8,8,3456]{2,1,0:T(8,128)(2,1)}, bf16[8,8,3456]{2,1,0:T(8,128)(2,1)S(1)}, u32[]{:S(2)}, u32[]{:S(2)}) collective-permute-start(bf16[8,8,3456]{2,1,0:T(8,128)(2,1)} %get-tuple-element.25), channel_id=1, source_target_pairs={{0,29},{1,30},{2,31},{3,0},{4,1},{5,2},{6,3},{7,4},{8,5},{9,6},{10... | collective-permute-start | bytes 1327112 | tf_op jit(solution)/shard_map/ppermute | solution.py:21
  170.1 43.5 %collective-permute-start.1 = (bf16[4,8,3456]{2,1,0:T(8,128)(2,1)}, bf16[4,8,3456]{2,1,0:T(8,128)(2,1)S(1)}, u32[]{:S(2)}, u32[]{:S(2)}) collective-permute-start(bf16[4,8,3456]{2,1,0:T(8,128)(2,1)} %get-tuple-element.24), channel_id=1, source_target_pairs={{0,28},{1,29},{2,30},{3,31},{4,0},{5,1},{6,2},{7,3},{8,4},{9,5},{1... | collective-permute-start | bytes 663560 | tf_op jit(solution)/shard_map/ppermute | solution.py:21
  172.0 65.9 %collective-permute-start.8 = (bf16[4,8,3456]{2,1,0:T(8,128)(2,1)}, bf16[4,8,3456]{2,1,0:T(8,128)(2,1)S(1)}, u32[]{:S(2)}, u32[]{:S(2)}) collective-permute-start(bf16[4,8,3456]{2,1,0:T(8,128)(2,1)} %get-tuple-element.32), channel_id=1, source_target_pairs={{0,4},{1,5},{2,6},{3,7},{4,8},{5,9},{6,10},{7,11},{8,12},{9,13},{1... | collective-permute-start | bytes 663560 | tf_op jit(solution)/shard_map/ppermute | solution.py:21
  179.9 62.1 %collective-permute-start.3 = (bf16[8,8,3456]{2,1,0:T(8,128)(2,1)}, bf16[8,8,3456]{2,1,0:T(8,128)(2,1)S(1)}, u32[]{:S(2)}, u32[]{:S(2)}) collective-permute-start(bf16[8,8,3456]{2,1,0:T(8,128)(2,1)} %get-tuple-element.26), channel_id=1, source_target_pairs={{0,30},{1,31},{2,0},{3,1},{4,2},{5,3},{6,4},{7,5},{8,6},{9,7},{10,... | collective-permute-start | bytes 1327112 | tf_op jit(solution)/shard_map/ppermute | solution.py:21
  182.0 68.2 %collective-permute-start.4 = (bf16[8,8,3456]{2,1,0:T(8,128)(2,1)}, bf16[8,8,3456]{2,1,0:T(8,128)(2,1)S(1)}, u32[]{:S(2)}, u32[]{:S(2)}) collective-permute-start(bf16[8,8,3456]{2,1,0:T(8,128)(2,1)} %get-tuple-element.27), channel_id=1, source_target_pairs={{0,31},{1,0},{2,1},{3,2},{4,3},{5,4},{6,5},{7,6},{8,7},{9,8},{10,9... | collective-permute-start | bytes 1327112 | tf_op jit(solution)/shard_map/ppermute | solution.py:21
  213.6 45.7 %collective-permute-start.5 = (bf16[8,8,3456]{2,1,0:T(8,128)(2,1)}, bf16[8,8,3456]{2,1,0:T(8,128)(2,1)S(1)}, u32[]{:S(2)}, u32[]{:S(2)}) collective-permute-start(bf16[8,8,3456]{2,1,0:T(8,128)(2,1)} %get-tuple-element.29), channel_id=1, source_target_pairs={{0,1},{1,2},{2,3},{3,4},{4,5},{5,6},{6,7},{7,8},{8,9},{9,10},{10,1... | collective-permute-start | bytes 1327112 | tf_op jit(solution)/shard_map/ppermute | solution.py:21
  238.0 39.7 %collective-permute-start.6 = (bf16[8,8,3456]{2,1,0:T(8,128)(2,1)}, bf16[8,8,3456]{2,1,0:T(8,128)(2,1)S(1)}, u32[]{:S(2)}, u32[]{:S(2)}) collective-permute-start(bf16[8,8,3456]{2,1,0:T(8,128)(2,1)} %get-tuple-element.30), channel_id=1, source_target_pairs={{0,2},{1,3},{2,4},{3,5},{4,6},{5,7},{6,8},{7,9},{8,10},{9,11},{10,... | collective-permute-start | bytes 1327112 | tf_op jit(solution)/shard_map/ppermute | solution.py:21
  239.9 54.2 %collective-permute-start.7 = (bf16[8,8,3456]{2,1,0:T(8,128)(2,1)}, bf16[8,8,3456]{2,1,0:T(8,128)(2,1)S(1)}, u32[]{:S(2)}, u32[]{:S(2)}) collective-permute-start(bf16[8,8,3456]{2,1,0:T(8,128)(2,1)} %get-tuple-element.31), channel_id=1, source_target_pairs={{0,3},{1,4},{2,5},{3,6},{4,7},{5,8},{6,9},{7,10},{8,11},{9,12},{10... | collective-permute-start | bytes 1327112 | tf_op jit(solution)/shard_map/ppermute | solution.py:21
  404.8 144.8 %all-to-all-start.2 = ((bf16[8,384,384]{2,1,0:T(8,128)(2,1)}), bf16[8,384,384]{2,1,0:T(8,128)(2,1)S(1)}, u32[]{:S(2)}, u32[]{:S(2)}) async-start(bf16[8,384,384]{2,1,0:T(8,128)(2,1)} %get-tuple-element.42), calls=%async_computation.2 | async-start | bytes 4718592 | tf_op jit(solution)/shard_map/all_to_all | solution.py:312
  408.6 69.6 %collective-permute-start = (f32[4,128]{1,0:T(4,128)S(1)}, f32[4,128]{1,0:T(4,128)S(1)}, u32[]{:S(2)}, u32[]{:S(2)}) collective-permute-start(f32[4,128]{1,0:T(4,128)S(1)} %pad_maximum_fusion.5), channel_id=1, source_target_pairs={{0,768},{256,0},{512,256},{768,512},{1,769},{257,1},{513,257},{769... | collective-permute-start | bytes 6152 | tf_op jit(solution)/shard_map/ppermute | solution.py:21
  410.9 92.1 %collective-permute-start.14 = (bf16[4,8,3584]{2,1,0:T(8,128)(2,1)}, bf16[4,8,3584]{2,1,0:T(8,128)(2,1)S(1)}, u32[]{:S(2)}, u32[]{:S(2)}) collective-permute-start(bf16[4,8,3584]{2,1,0:T(8,128)(2,1)} %get-tuple-element.34), channel_id=1, source_target_pairs={{0,771},{1,772},{2,773},{3,774},{4,775},{5,776},{6,777},{7,778},{8... | collective-permute-start | bytes 688136 | tf_op jit(solution)/shard_map/ppermute | solution.py:31
  420.7 88.7 %collective-permute-start.15 = (bf16[4,8,3584]{2,1,0:T(8,128)(2,1)}, bf16[4,8,3584]{2,1,0:T(8,128)(2,1)S(1)}, u32[]{:S(2)}, u32[]{:S(2)}) collective-permute-start(bf16[4,8,3584]{2,1,0:T(8,128)(2,1)} %get-tuple-element.35), channel_id=1, source_target_pairs={{0,770},{1,771},{2,772},{3,773},{4,774},{5,775},{6,776},{7,777},{8... | collective-permute-start | bytes 688136 | tf_op jit(solution)/shard_map/ppermute | solution.py:31
  426.9 48.7 %collective-permute-start.24 = (bf16[192,384]{1,0:T(8,128)(2,1)S(1)}, bf16[192,384]{1,0:T(8,128)(2,1)S(1)}, u32[]{:S(2)}, u32[]{:S(2)}) collective-permute-start(bf16[192,384]{1,0:T(8,128)(2,1)S(1)} %get-tuple-element.50), channel_id=1, source_target_pairs={{0,24},{1,25},{2,26},{3,27},{4,28},{5,29},{6,30},{7,31},{8,0},{9,1... | collective-permute-start | bytes 442376 | tf_op jit(solution)/shard_map/ppermute | solution.py:21
  450.7 64.7 %collective-permute-start.16 = (bf16[4,8,3584]{2,1,0:T(8,128)(2,1)S(1)}, bf16[4,8,3584]{2,1,0:T(8,128)(2,1)S(1)}, u32[]{:S(2)}, u32[]{:S(2)}) collective-permute-start(bf16[4,8,3584]{2,1,0:T(8,128)(2,1)S(1)} %copy-done.22), channel_id=1, source_target_pairs={{0,769},{1,770},{2,771},{3,772},{4,773},{5,774},{6,775},{7,776},{8... | collective-permute-start | bytes 688136 | tf_op jit(solution)/shard_map/ppermute | solution.py:31
  478.2 47.9 %collective-permute-start.17 = (bf16[4,8,3584]{2,1,0:T(8,128)(2,1)S(1)}, bf16[4,8,3584]{2,1,0:T(8,128)(2,1)S(1)}, u32[]{:S(2)}, u32[]{:S(2)}) collective-permute-start(bf16[4,8,3584]{2,1,0:T(8,128)(2,1)S(1)} %copy-done.21), channel_id=1, source_target_pairs={{0,768},{1,769},{2,770},{3,771},{4,772},{5,773},{6,774},{7,775},{8... | collective-permute-start | bytes 688136 | tf_op jit(solution)/shard_map/ppermute | solution.py:31
  501.2 29.4 %collective-permute-start.18 = (bf16[4,8,3584]{2,1,0:T(8,128)(2,1)S(1)}, bf16[4,8,3584]{2,1,0:T(8,128)(2,1)}, u32[]{:S(2)}, u32[]{:S(2)}) collective-permute-start(bf16[4,8,3584]{2,1,0:T(8,128)(2,1)S(1)} %copy-done.20), channel_id=1, source_target_pairs={{0,799},{1,768},{2,769},{3,770},{4,771},{5,772},{6,773},{7,774},{8... | collective-permute-start | bytes 688136 | tf_op jit(solution)/shard_map/ppermute | solution.py:31
  503.1 27.5 %collective-permute-start.19 = (bf16[4,8,3584]{2,1,0:T(8,128)(2,1)S(1)}, bf16[4,8,3584]{2,1,0:T(8,128)(2,1)}, u32[]{:S(2)}, u32[]{:S(2)}) collective-permute-start(bf16[4,8,3584]{2,1,0:T(8,128)(2,1)S(1)} %copy-done.19), channel_id=1, source_target_pairs={{0,798},{1,799},{2,768},{3,769},{4,770},{5,771},{6,772},{7,773},{8... | collective-permute-start | bytes 688136 | tf_op jit(solution)/shard_map/ppermute | solution.py:31
  515.4 35.1 %collective-permute-start.23 = (bf16[384,384]{1,0:T(8,128)(2,1)}, bf16[384,384]{1,0:T(8,128)(2,1)}, u32[]{:S(2)}, u32[]{:S(2)}) collective-permute-start(bf16[384,384]{1,0:T(8,128)(2,1)} %pad_maximum_fusion.3), channel_id=1, source_target_pairs={{0,8},{1,9},{2,10},{3,11},{4,12},{5,13},{6,14},{7,15},{8,16},{9,17... | collective-permute-start | bytes 884744 | tf_op jit(solution)/shard_map/ppermute | solution.py:21
  526.1 69.3 %collective-permute-start.25 = (bf16[384,384]{1,0:T(8,128)(2,1)}, bf16[384,384]{1,0:T(8,128)(2,1)}, u32[]{:S(2)}, u32[]{:S(2)}) collective-permute-start(bf16[384,384]{1,0:T(8,128)(2,1)} %pad_maximum_fusion.4), channel_id=1, source_target_pairs={{0,24},{1,25},{2,26},{3,27},{4,28},{5,29},{6,30},{7,31},{8,0},{9,1... | collective-permute-start | bytes 884744 | tf_op jit(solution)/shard_map/ppermute | solution.py:21
  (31 other events, 972.1 us)

commit v3 on v2

--- a/solution.py
+++ b/solution.py
@@ -14,6 +14,7 @@
 
 
 COPIES = 4
+CORES = 2
 
 
 def shifted(value, axis, steps):
@@ -130,13 +131,15 @@
 def expert_kernel(*refs, experts):
     reach = experts // (2 * COPIES)
     offsets = offsets_of(reach)
+    core_ref, refs = refs[0], refs[1:]
     arrived = refs[: len(offsets)]
     own_w = refs[len(offsets) : len(offsets) + 3]
     side_w, far_w = refs[len(offsets) + 3 : len(offsets) + 5]
     at = len(offsets) + 5
     returned = refs[at : at + len(offsets)]
-    own_t, side_t, far_t = refs[at + len(offsets) : at + len(offsets) + 3]
-    x_ref, g_ref, folded = refs[at + len(offsets) + 3 :]
+    at += len(offsets)
+    far_keep, far_give, side_keep, side_give, own_keep, own_give = refs[at : at + 6]
+    x_ref, g_ref, folded = refs[at + 6 :]
     width = own_w[0].shape[0]
     ff = own_w[0].shape[1]
     fold = width // SUB
@@ -157,9 +160,9 @@
         if k == 0:
             gate_w, up_w, down_w = [w[...] for w in own_w]
         elif k == 2:
-            gate_w, up_w, down_w = [far_w[:, i].reshape(width, ff) for i in range(3)]
+            gate_w, up_w, down_w = [far_w[:, :, 0, i].reshape(width, ff) for i in range(3)]
         else:
-            gate_w, up_w, down_w = [side_w[:, k // 2, i].reshape(width, ff) for i in range(3)]
+            gate_w, up_w, down_w = [side_w[:, :, k // 2, i].reshape(width, ff) for i in range(3)]
         x = x_ref[0:rows, :]
         g = g_ref[0:rows, :]
         gate = jnp.dot(x, gate_w, preferred_element_type=F32)
@@ -195,33 +198,39 @@
         for i, (left, right) in enumerate(((x, d_gate), (x, d_up), (g, hidden))):
             cols = slice(i * ff, (i + 1) * ff)
             term = lax.dot_general(left, right, by_rows, preferred_element_type=F32).astype(BF16)
-            if k == 0:
-                own_t[:, :, cols] = term.reshape(own_t.shape[0], -1, ff)
-            elif k == 2:
-                far_t[:, :, cols] = term.reshape(far_t.shape[0], -1, ff)
-            else:
-                side_t[:, k // 2, :, cols] = term.reshape(side_t.shape[0], -1, ff)
-
-
-def run_experts(arrived, own_w, side_w, far_w, experts):
+            chips = far_keep.shape[0]
+            term = term.reshape(chips, CORES, -1, ff)
+            at = k // 2 if k % 2 else 0
+            keep, give = ((own_keep, own_give), (side_keep, side_give), (far_keep, far_give))[
+                1 if k % 2 else k
+            ]
+            for core in range(CORES):
+
+                @pl.when(core_ref[0] == core)
+                def _(term=term, core=core, keep=keep, give=give, at=at, cols=cols):
+                    keep[:, at, :, cols] = term[:, core]
+                    give[:, at, :, cols] = term[:, 1 - core]
+
+
+def run_experts(core, arrived, own_w, side_w, far_w, experts):
     reach = experts // (2 * COPIES)
     width, ff = own_w[0].shape
     fold = width // SUB
-    replicas = far_w.shape[0]
+    chips = far_w.shape[1]
     vmem = pl.BlockSpec(memory_space=pltpu.VMEM)
     shapes = [
         jax.ShapeDtypeStruct((len(blocks_of(d, reach)), SUB, width + fold + EXTRA), BF16)
         for d in offsets_of(reach)
     ] + [
-        jax.ShapeDtypeStruct((replicas,) + lead + (width // replicas, 3 * ff), BF16)
-        for lead in ((), (2,), ())
+        jax.ShapeDtypeStruct((chips, hosts, width // (CORES * chips), 3 * ff), BF16)
+        for hosts in (1, 1, 2, 2, 1, 1)
     ]
     count = 2 * reach + 1
     rows = count * SUB + -(-count // SUB) * SUB
     outs = pl.pallas_call(
         lambda *refs: expert_kernel(*refs, experts=experts),
         out_shape=shapes,
-        in_specs=[vmem] * (len(arrived) + 5),
+        in_specs=[pl.BlockSpec(memory_space=pltpu.SMEM)] + [vmem] * (len(arrived) + 5),
         out_specs=[vmem] * len(shapes),
         scratch_shapes=[
             pltpu.VMEM((rows, width), BF16),
@@ -230,8 +239,8 @@
         ],
         name="experts",
         interpret=INTERPRET,
-    )(*arrived, *own_w, side_w, far_w)
-    return outs[:-3], outs[-3:]
+    )(core, *arrived, *own_w, side_w, far_w)
+    return outs[:-6], outs[-6:]
 
 
 def scalars_kernel(here_ref, routes_ref, combine_ref, *refs, experts):
@@ -303,14 +312,16 @@
     )(here, routes_t, *arrived)
 
 
-def spread_over(x, axis):
-    copies = jnp.broadcast_to(x[None], (lax.axis_size(axis),) + x.shape)
-    return lax.all_to_all(copies, axis, split_axis=0, concat_axis=0, tiled=True)
-
-
-def summed_on_arrival(pieces, axis):
-    arrived = lax.all_to_all(pieces, axis, split_axis=0, concat_axis=0, tiled=True)
-    return arrived.astype(F32).sum(axis=0)
+def over_chips(x):
+    count = lax.axis_size("dp")
+    groups = [list(range(c, count, CORES)) for c in range(CORES)]
+    return lax.all_to_all(
+        x, "dp", split_axis=0, concat_axis=0, tiled=True, axis_index_groups=groups
+    )
+
+
+def other_core(x):
+    return lax.ppermute(x, "dp", [(i, i ^ 1) for i in range(lax.axis_size("dp"))])
 
 
 def per_device(tokens_in, upstream, routes, combine, gate_proj, up_proj, down_proj):
@@ -326,34 +337,53 @@
     combine_t = combine[0].T
     own_w = [w[0, 0] for w in (gate_proj, up_proj, down_proj)]
     part = width // replicas
-    start = lax.axis_index("dp") * part
+    chips = replicas // CORES
+    lane = lax.axis_index("dp")
+    core = (lane % CORES).astype(jnp.int32)
+    start = (core * chips + lane // CORES) * part
     offsets = offsets_of(reach)
+
+    def spread(x):
+        same = over_chips(jnp.broadcast_to(x[None], (chips,) + x.shape))
+        other = other_core(same)
+        low = jnp.where(core == 0, same, other)
+        high = jnp.where(core == 0, other, same)
+        return jnp.stack([low, high])
+
     piece = jnp.stack([lax.dynamic_slice_in_dim(w, start, part, 0) for w in own_w])
     side1 = shifted(piece, "expert", -period)
     side3 = shifted(piece, "expert", period)
     low = shifted(side1[:, : part // 2], "expert", -period)
     high = shifted(side3[:, part // 2 :], "expert", period)
-    side_w = spread_over(jnp.stack([side1, side3]), "dp")
-    far_w = spread_over(jnp.concatenate([low, high], axis=1), "dp")
+    side_w = spread(jnp.stack([side1, side3]))
+    far_w = spread(jnp.concatenate([low, high], axis=1)[None])
     packed = pack(here, routes_t, combine_t, tokens_in[0], upstream[0], experts)
     behind = shifted(jnp.concatenate([routes_t.astype(F32), combine_t.astype(F32)]), "section", -1)
     arrived = list(packed)
     for i, d in enumerate(offsets):
         if d:
             arrived[i] = shifted(packed[i], "expert", d)
-    done, (own_t, side_t, far_t) = run_experts(arrived, own_w, side_w, far_w, experts)
+    done, terms = run_experts(
+        core.reshape(1), arrived, own_w, side_w, far_w, experts
+    )
     back = []
     for i, d in enumerate(offsets):
         back.append(sent_back(done[i], -d))
-    far_sum = summed_on_arrival(far_t, "dp").astype(BF16)
+
+    def summed(keep, give):
+        got = other_core(give)
+        both = (keep.astype(F32) + got.astype(F32)).astype(BF16)
+        return over_chips(both).astype(F32).sum(axis=0)
+
+    far_sum = summed(*terms[0:2])[0].astype(BF16)
+    side_sum = summed(*terms[2:4])
+    own_sum = summed(*terms[4:6])[0]
     low = shifted(far_sum[: part // 2], "expert", period)
     high = shifted(far_sum[part // 2 :], "expert", -period)
-    side_sum = summed_on_arrival(side_t, "dp")
     joined = jnp.concatenate([side_sum[0, : part // 2] + low.astype(F32), side_sum[0, part // 2 :]])
     side1 = shifted(joined.astype(BF16), "expert", period)
     joined = jnp.concatenate([side_sum[1, : part // 2], side_sum[1, part // 2 :] + high.astype(F32)])
     side3 = shifted(joined.astype(BF16), "expert", -period)
-    own_sum = summed_on_arrival(own_t, "dp")
     weight_grad = (own_sum + side1.astype(F32) + side3.astype(F32)) * (1.0 / replicas)
     routes_b = behind[:2].astype(jnp.int32)
     combine_grad = unpack_scalars(here, routes_b, behind[2:], back, width, experts)

time: 599 us -> 551 us (0.920)
  the two profiles are of different devices: /device:TPU:104 before, /device:TPU:2 now
where the time goes in v3:
time: 551 us; the launch traced here: 549 us
  waiting for transfers between devices  276 us (50%)
  starting transfers between devices  209 us (38%)
  Pallas kernels  33 us (6%)
  other arithmetic  22.3 us (4%)
  local copies, waits for them, and re-layouts  8.05 us (1%)
    ppermute x18, waiting for transfers between devices, shifted(): lax.ppermute(value, axis, [(s, (s + steps) % count) for s in range(count)])  185 us
    ppermute x18, starting transfers between devices, shifted(): lax.ppermute(value, axis, [(s, (s + steps) % count) for s in range(count)])  124 us
    ppermute x9, waiting for transfers between devices, sent_back(): return lax.ppermute(value, ('section', 'expert'), pairs)  61.8 us
    ppermute x9, starting transfers between devices, sent_back(): return lax.ppermute(value, ('section', 'expert'), pairs)  50.6 us
    all_to_all x5, waiting for transfers between devices, over_chips(): lax.all_to_all(x, 'dp', split_axis=0, concat_axis=0, tiled=True, axis_ind...  25.2 us
    all_to_all x5, starting transfers between devices, over_chips(): lax.all_to_all(x, 'dp', split_axis=0, concat_axis=0, tiled=True, axis_ind...  24.5 us
    pallas_call x1, Pallas kernels, run_experts(): pl.pallas_call(lambda *refs: expert_kernel(*refs, experts=experts), out_s...  22.8 us
  transfers between devices with their start and end apart: 37, of which 16 were waited for; matrix products, arithmetic and copies ran while one was open for 4% of the time, Pallas kernels for 2%

profile of v3, /device:TPU:2, one launch (start us, length us, event | category | flops | bytes accessed | tf_op | source)
XLA Modules:
  0.0 549.4 jit_solution(15466044100223783755)
XLA Ops:
  2.6 23.0 %collective-permute-start.9 = (bf16[3,384,128]{2,1,0:T(8,128)(2,1)S(1)}, bf16[3,384,128]{2,1,0:T(8,128)(2,1)S(1)}, u32[]{:S(2)}, u32[]{:S(2)}) collective-permute-start(bf16[3,384,128]{2,1,0:T(8,128)(2,1)S(1)} %pad_maximum_fusion.3), channel_id=1, source_target_pairs={{0,24},{1,25},{2,26},{3,27},{4,28},{5,29},{6,30},{7,31},{8,0},{9,1... | collective-permute-start | bytes 884744 | tf_op jit(solution)/shard_map/ppermute | solution.py:22
  27.5 48.8 %collective-permute-done.9 = bf16[3,384,128]{2,1,0:T(8,128)(2,1)S(1)} collective-permute-done((bf16[3,384,128]{2,1,0:T(8,128)(2,1)S(1)}, bf16[3,384,128]{2,1,0:T(8,128)(2,1)S(1)}, u32[]{:S(2)}, u32[]{:S(2)}) %collective-permute-start.9) | collective-permute-done | bytes 294944 | tf_op jit(solution)/shard_map/ppermute | solution.py:22
  83.1 13.1 %collective-permute-start.12 = (bf16[3,192,128]{2,1,0:T(8,128)(2,1)S(1)}, bf16[3,192,128]{2,1,0:T(8,128)(2,1)S(1)}, u32[]{:S(2)}, u32[]{:S(2)}) collective-permute-start(bf16[3,192,128]{2,1,0:T(8,128)(2,1)S(1)} %slice.42), channel_id=1, source_target_pairs={{0,24},{1,25},{2,26},{3,27},{4,28},{5,29},{6,30},{7,31},{8,0},{9,1... | collective-permute-start | bytes 442376 | tf_op jit(solution)/shard_map/ppermute | solution.py:22
  98.1 8.7 %collective-permute-done.12 = bf16[3,192,128]{2,1,0:T(8,128)(2,1)S(1)} collective-permute-done((bf16[3,192,128]{2,1,0:T(8,128)(2,1)S(1)}, bf16[3,192,128]{2,1,0:T(8,128)(2,1)S(1)}, u32[]{:S(2)}, u32[]{:S(2)}) %collective-permute-start.12) | collective-permute-done | bytes 147488 | tf_op jit(solution)/shard_map/ppermute | solution.py:22
  106.9 14.8 %collective-permute-done.13 = bf16[3,192,128]{2,1,0:T(8,128)(2,1)S(1)} collective-permute-done((bf16[3,192,128]{2,1,0:T(8,128)(2,1)S(1)}, bf16[3,192,128]{2,1,0:T(8,128)(2,1)S(1)}, u32[]{:S(2)}, u32[]{:S(2)}) %collective-permute-start.13) | collective-permute-done | bytes 147488 | tf_op jit(solution)/shard_map/ppermute | solution.py:22
  129.7 13.2 %all-to-all-done.1 = bf16[4,1,3,384,128]{4,3,2,1,0:T(8,128)(2,1)S(1)} async-done(((bf16[4,1,3,384,128]{4,3,2,1,0:T(8,128)(2,1)}), bf16[4,1,3,384,128]{4,3,2,1,0:T(8,128)(2,1)S(1)}, u32[]{:S(2)}, u32[]{:S(2)}) %all-to-all-start.1) | async-done | bytes 1179680 | tf_op jit(solution)/shard_map/all_to_all | solution.py:318
  151.8 9.0 %collective-permute-start.3 = (bf16[8,8,3456]{2,1,0:T(8,128)(2,1)}, bf16[8,8,3456]{2,1,0:T(8,128)(2,1)}, u32[]{:S(2)}, u32[]{:S(2)}) collective-permute-start(bf16[8,8,3456]{2,1,0:T(8,128)(2,1)} %get-tuple-element.29), channel_id=1, source_target_pairs={{0,30},{1,31},{2,0},{3,1},{4,2},{5,3},{6,4},{7,5},{8,6},{9,7},{10,... | collective-permute-start | bytes 1327112 | tf_op jit(solution)/shard_map/ppermute | solution.py:22
  164.6 6.6 %collective-permute-start.8 = (bf16[4,8,3456]{2,1,0:T(8,128)(2,1)}, bf16[4,8,3456]{2,1,0:T(8,128)(2,1)S(1)}, u32[]{:S(2)}, u32[]{:S(2)}) collective-permute-start(bf16[4,8,3456]{2,1,0:T(8,128)(2,1)} %get-tuple-element.35), channel_id=1, source_target_pairs={{0,4},{1,5},{2,6},{3,7},{4,8},{5,9},{6,10},{7,11},{8,12},{9,13},{1... | collective-permute-start | bytes 663560 | tf_op jit(solution)/shard_map/ppermute | solution.py:22
  174.3 41.2 %collective-permute-done.1.refs_1_ = bf16[4,8,3456]{2,1,0:T(8,128)(2,1)} collective-permute-done((bf16[4,8,3456]{2,1,0:T(8,128)(2,1)}, bf16[4,8,3456]{2,1,0:T(8,128)(2,1)}, u32[]{:S(2)}, u32[]{:S(2)}) %collective-permute-start.1) | collective-permute-done | bytes 221216 | tf_op jit(solution)/shard_map/ppermute | solution.py:22
  221.4 17.9 %collective-permute-start.6 = (bf16[8,8,3456]{2,1,0:T(8,128)(2,1)S(1)}, bf16[8,8,3456]{2,1,0:T(8,128)(2,1)}, u32[]{:S(2)}, u32[]{:S(2)}) collective-permute-start(bf16[8,8,3456]{2,1,0:T(8,128)(2,1)S(1)} %copy-done.14), channel_id=1, source_target_pairs={{0,2},{1,3},{2,4},{3,5},{4,6},{5,7},{6,8},{7,9},{8,10},{9,11},{10,... | collective-permute-start | bytes 1327112 | tf_op jit(solution)/shard_map/ppermute | solution.py:22
  250.1 15.4 %collective-permute-done.6.refs_7_ = bf16[8,8,3456]{2,1,0:T(8,128)(2,1)} collective-permute-done((bf16[8,8,3456]{2,1,0:T(8,128)(2,1)S(1)}, bf16[8,8,3456]{2,1,0:T(8,128)(2,1)}, u32[]{:S(2)}, u32[]{:S(2)}) %collective-permute-start.6) | collective-permute-done | bytes 442400 | tf_op jit(solution)/shard_map/ppermute | solution.py:22
  265.5 30.5 %collective-permute-done.7.refs_8_ = bf16[8,8,3456]{2,1,0:T(8,128)(2,1)} collective-permute-done((bf16[8,8,3456]{2,1,0:T(8,128)(2,1)S(1)}, bf16[8,8,3456]{2,1,0:T(8,128)(2,1)}, u32[]{:S(2)}, u32[]{:S(2)}) %collective-permute-start.7) | collective-permute-done | bytes 442400 | tf_op jit(solution)/shard_map/ppermute | solution.py:22
  296.1 22.8 %experts.1 = (bf16[2,8,3584]{2,1,0:T(8,128)(2,1)}, bf16[4,8,3584]{2,1,0:T(8,128)(2,1)}, bf16[4,8,3584]{2,1,0:T(8,128)(2,1)}, bf16[4,8,3584]{2,1,0:T(8,128)(2,1)}...) custom-call(s32[1]{0:T(128)} %bitcast.5.refs_0_, ...), custom_call_target="tpu_custom_call" | custom-call | tf_op jit(solution)/shard_map/experts/pallas_call | solution.py:230
  338.6 12.0 %all-to-all-done.4 = bf16[4,1,384,384]{3,2,1,0:T(8,128)(2,1)S(1)} async-done(((bf16[4,1,384,384]{3,2,1,0:T(8,128)(2,1)}), bf16[4,1,384,384]{3,2,1,0:T(8,128)(2,1)S(1)}, u32[]{:S(2)}, u32[]{:S(2)}) %all-to-all-start.4) | async-done | bytes 1179680 | tf_op jit(solution)/shard_map/all_to_all | solution.py:318
  364.4 5.5 %collective-permute-start.17 = (bf16[4,8,3584]{2,1,0:T(8,128)(2,1)}, bf16[4,8,3584]{2,1,0:T(8,128)(2,1)}, u32[]{:S(2)}, u32[]{:S(2)}) collective-permute-start(bf16[4,8,3584]{2,1,0:T(8,128)(2,1)} %get-tuple-element.38), channel_id=1, source_target_pairs={{0,770},{1,771},{2,772},{3,773},{4,774},{5,775},{6,776},{7,777},{8... | collective-permute-start | bytes 688136 | tf_op jit(solution)/shard_map/ppermute | solution.py:32
  377.2 12.6 %collective-permute-start.29 = (bf16[192,384]{1,0:T(8,128)(2,1)}, bf16[192,384]{1,0:T(8,128)(2,1)}, u32[]{:S(2)}, u32[]{:S(2)}) collective-permute-start(bf16[192,384]{1,0:T(8,128)(2,1)} %get-tuple-element.60), channel_id=1, source_target_pairs={{0,24},{1,25},{2,26},{3,27},{4,28},{5,29},{6,30},{7,31},{8,0},{9,1... | collective-permute-start | bytes 442376 | tf_op jit(solution)/shard_map/ppermute | solution.py:22
  395.1 7.9 %collective-permute-done.27 = bf16[192,384]{1,0:T(8,128)(2,1)} collective-permute-done((bf16[192,384]{1,0:T(8,128)(2,1)}, bf16[192,384]{1,0:T(8,128)(2,1)}, u32[]{:S(2)}, u32[]{:S(2)}) %collective-permute-start.27) | collective-permute-done | bytes 147488 | tf_op jit(solution)/shard_map/ppermute | solution.py:22
  403.0 13.6 %collective-permute-start.18 = (bf16[4,8,3584]{2,1,0:T(8,128)(2,1)S(1)}, bf16[4,8,3584]{2,1,0:T(8,128)(2,1)S(1)}, u32[]{:S(2)}, u32[]{:S(2)}) collective-permute-start(bf16[4,8,3584]{2,1,0:T(8,128)(2,1)S(1)} %copy-done.21), channel_id=1, source_target_pairs={{0,769},{1,770},{2,771},{3,772},{4,773},{5,774},{6,775},{7,776},{8... | collective-permute-start | bytes 688136 | tf_op jit(solution)/shard_map/ppermute | solution.py:32
  419.7 6.4 %collective-permute-start.19 = (bf16[4,8,3584]{2,1,0:T(8,128)(2,1)S(1)}, bf16[4,8,3584]{2,1,0:T(8,128)(2,1)S(1)}, u32[]{:S(2)}, u32[]{:S(2)}) collective-permute-start(bf16[4,8,3584]{2,1,0:T(8,128)(2,1)S(1)} %copy-done.20), channel_id=1, source_target_pairs={{0,768},{1,769},{2,770},{3,771},{4,772},{5,773},{6,774},{7,775},{8... | collective-permute-start | bytes 688136 | tf_op jit(solution)/shard_map/ppermute | solution.py:32
  432.8 9.5 %collective-permute-done.23.refs_10_.refs_11_ = bf16[2,8,3584]{2,1,0:T(8,128)(2,1)S(1)} collective-permute-done((bf16[2,8,3584]{2,1,0:T(8,128)(2,1)S(1)}, bf16[2,8,3584]{2,1,0:T(8,128)(2,1)S(1)}, u32[]{:S(2)}, u32[]{:S(2)}) %collective-permute-start.23) | collective-permute-done | bytes 114720 | tf_op jit(solution)/shard_map/ppermute | solution.py:32
  442.4 13.2 %collective-permute-start.20 = (bf16[4,8,3584]{2,1,0:T(8,128)(2,1)S(1)}, bf16[4,8,3584]{2,1,0:T(8,128)(2,1)S(1)}, u32[]{:S(2)}, u32[]{:S(2)}) collective-permute-start(bf16[4,8,3584]{2,1,0:T(8,128)(2,1)S(1)} %copy-done.19), channel_id=1, source_target_pairs={{0,799},{1,768},{2,769},{3,770},{4,771},{5,772},{6,773},{7,774},{8... | collective-permute-start | bytes 688136 | tf_op jit(solution)/shard_map/ppermute | solution.py:32
  462.5 13.5 %collective-permute-start.28 = (bf16[384,384]{1,0:T(8,128)(2,1)S(1)}, bf16[384,384]{1,0:T(8,128)(2,1)S(1)}, u32[]{:S(2)}, u32[]{:S(2)}) collective-permute-start(bf16[384,384]{1,0:T(8,128)(2,1)S(1)} %pad_maximum_fusion.5), channel_id=1, source_target_pairs={{0,8},{1,9},{2,10},{3,11},{4,12},{5,13},{6,14},{7,15},{8,16},{9,17... | collective-permute-start | bytes 884744 | tf_op jit(solution)/shard_map/ppermute | solution.py:22
  478.6 47.4 %collective-permute-done.22.refs_9_.refs_10_ = bf16[4,8,3584]{2,1,0:T(8,128)(2,1)S(1)} collective-permute-done((bf16[4,8,3584]{2,1,0:T(8,128)(2,1)S(1)}, bf16[4,8,3584]{2,1,0:T(8,128)(2,1)S(1)}, u32[]{:S(2)}, u32[]{:S(2)}) %collective-permute-start.22) | collective-permute-done | bytes 229408 | tf_op jit(solution)/shard_map/ppermute | solution.py:32
  535.9 12.1 %collective-permute-done.30 = bf16[384,384]{1,0:T(8,128)(2,1)S(1)} collective-permute-done((bf16[384,384]{1,0:T(8,128)(2,1)}, bf16[384,384]{1,0:T(8,128)(2,1)S(1)}, u32[]{:S(2)}, u32[]{:S(2)}) %collective-permute-start.30) | collective-permute-done | bytes 294944 | tf_op jit(solution)/shard_map/ppermute | solution.py:22
  (134 shorter events, 129.3 us)
Async XLA Ops:
  2.6 73.7 %collective-permute-start.9 = (bf16[3,384,128]{2,1,0:T(8,128)(2,1)S(1)}, bf16[3,384,128]{2,1,0:T(8,128)(2,1)S(1)}, u32[]{:S(2)}, u32[]{:S(2)}) collective-permute-start(bf16[3,384,128]{2,1,0:T(8,128)(2,1)S(1)} %pad_maximum_fusion.3), channel_id=1, source_target_pairs={{0,24},{1,25},{2,26},{3,27},{4,28},{5,29},{6,30},{7,31},{8,0},{9,1... | collective-permute-start | bytes 884744 | tf_op jit(solution)/shard_map/ppermute | solution.py:22
  25.6 50.7 %collective-permute-start.10 = (bf16[3,384,128]{2,1,0:T(8,128)(2,1)S(1)}, bf16[3,384,128]{2,1,0:T(8,128)(2,1)S(1)}, u32[]{:S(2)}, u32[]{:S(2)}) collective-permute-start(bf16[3,384,128]{2,1,0:T(8,128)(2,1)S(1)} %pad_maximum_fusion.3), channel_id=1, source_target_pairs={{0,8},{1,9},{2,10},{3,11},{4,12},{5,13},{6,14},{7,15},{8,16},{9,17... | collective-permute-start | bytes 884744 | tf_op jit(solution)/shard_map/ppermute | solution.py:22
  78.3 43.4 %all-to-all-start = ((bf16[4,2,3,384,128]{4,3,2,1,0:T(8,128)(2,1)}), bf16[4,2,3,384,128]{4,3,2,1,0:T(8,128)(2,1)S(1)}, u32[]{:S(2)}, u32[]{:S(2)}) async-start(bf16[4,2,3,384,128]{4,3,2,1,0:T(8,128)(2,1)} %broadcast_in_dim.20), calls=%async_computation | async-start | bytes 4718592 | tf_op jit(solution)/shard_map/all_to_all | solution.py:318
  127.7 111.5 %collective-permute-start.11 = (bf16[4,2,3,384,128]{4,3,2,1,0:T(8,128)(2,1)S(1)}, bf16[4,2,3,384,128]{4,3,2,1,0:T(8,128)(2,1)}, u32[]{:S(2)}, u32[]{:S(2)}) collective-permute-start(bf16[4,2,3,384,128]{4,3,2,1,0:T(8,128)(2,1)S(1)} %all-to-all-done), channel_id=1, source_target_pairs={{0,32},{32,0},{64,96},{96,64},{128,160},{160,128},{192,224},{224,1... | collective-permute-start | bytes 7077896 | tf_op jit(solution)/shard_map/ppermute | solution.py:324
  149.9 71.4 %collective-permute-start.2 = (bf16[8,8,3456]{2,1,0:T(8,128)(2,1)}, bf16[8,8,3456]{2,1,0:T(8,128)(2,1)}, u32[]{:S(2)}, u32[]{:S(2)}) collective-permute-start(bf16[8,8,3456]{2,1,0:T(8,128)(2,1)} %get-tuple-element.28), channel_id=1, source_target_pairs={{0,29},{1,30},{2,31},{3,0},{4,1},{5,2},{6,3},{7,4},{8,5},{9,6},{10... | collective-permute-start | bytes 1327112 | tf_op jit(solution)/shard_map/ppermute | solution.py:22
  151.8 94.0 %collective-permute-start.3 = (bf16[8,8,3456]{2,1,0:T(8,128)(2,1)}, bf16[8,8,3456]{2,1,0:T(8,128)(2,1)}, u32[]{:S(2)}, u32[]{:S(2)}) collective-permute-start(bf16[8,8,3456]{2,1,0:T(8,128)(2,1)} %get-tuple-element.29), channel_id=1, source_target_pairs={{0,30},{1,31},{2,0},{3,1},{4,2},{5,3},{6,4},{7,5},{8,6},{9,7},{10,... | collective-permute-start | bytes 1327112 | tf_op jit(solution)/shard_map/ppermute | solution.py:22
  160.9 54.6 %collective-permute-start.1 = (bf16[4,8,3456]{2,1,0:T(8,128)(2,1)}, bf16[4,8,3456]{2,1,0:T(8,128)(2,1)}, u32[]{:S(2)}, u32[]{:S(2)}) collective-permute-start(bf16[4,8,3456]{2,1,0:T(8,128)(2,1)} %get-tuple-element.27), channel_id=1, source_target_pairs={{0,28},{1,29},{2,30},{3,31},{4,0},{5,1},{6,2},{7,3},{8,4},{9,5},{1... | collective-permute-start | bytes 663560 | tf_op jit(solution)/shard_map/ppermute | solution.py:22
  164.6 53.1 %collective-permute-start.8 = (bf16[4,8,3456]{2,1,0:T(8,128)(2,1)}, bf16[4,8,3456]{2,1,0:T(8,128)(2,1)S(1)}, u32[]{:S(2)}, u32[]{:S(2)}) collective-permute-start(bf16[4,8,3456]{2,1,0:T(8,128)(2,1)} %get-tuple-element.35), channel_id=1, source_target_pairs={{0,4},{1,5},{2,6},{3,7},{4,8},{5,9},{6,10},{7,11},{8,12},{9,13},{1... | collective-permute-start | bytes 663560 | tf_op jit(solution)/shard_map/ppermute | solution.py:22
  215.5 30.4 %collective-permute-start.4 = (bf16[8,8,3456]{2,1,0:T(8,128)(2,1)S(1)}, bf16[8,8,3456]{2,1,0:T(8,128)(2,1)S(1)}, u32[]{:S(2)}, u32[]{:S(2)}) collective-permute-start(bf16[8,8,3456]{2,1,0:T(8,128)(2,1)S(1)} %copy-done.16), channel_id=1, source_target_pairs={{0,31},{1,0},{2,1},{3,2},{4,3},{5,4},{6,5},{7,6},{8,7},{9,8},{10,9... | collective-permute-start | bytes 1327112 | tf_op jit(solution)/shard_map/ppermute | solution.py:22
  217.8 32.3 %collective-permute-start.5 = (bf16[8,8,3456]{2,1,0:T(8,128)(2,1)S(1)}, bf16[8,8,3456]{2,1,0:T(8,128)(2,1)S(1)}, u32[]{:S(2)}, u32[]{:S(2)}) collective-permute-start(bf16[8,8,3456]{2,1,0:T(8,128)(2,1)S(1)} %copy-done.15), channel_id=1, source_target_pairs={{0,1},{1,2},{2,3},{3,4},{4,5},{5,6},{6,7},{7,8},{8,9},{9,10},{10,1... | collective-permute-start | bytes 1327112 | tf_op jit(solution)/shard_map/ppermute | solution.py:22
  221.4 44.2 %collective-permute-start.6 = (bf16[8,8,3456]{2,1,0:T(8,128)(2,1)S(1)}, bf16[8,8,3456]{2,1,0:T(8,128)(2,1)}, u32[]{:S(2)}, u32[]{:S(2)}) collective-permute-start(bf16[8,8,3456]{2,1,0:T(8,128)(2,1)S(1)} %copy-done.14), channel_id=1, source_target_pairs={{0,2},{1,3},{2,4},{3,5},{4,6},{5,7},{6,8},{7,9},{8,10},{9,11},{10,... | collective-permute-start | bytes 1327112 | tf_op jit(solution)/shard_map/ppermute | solution.py:22
  239.3 56.8 %collective-permute-start.7 = (bf16[8,8,3456]{2,1,0:T(8,128)(2,1)S(1)}, bf16[8,8,3456]{2,1,0:T(8,128)(2,1)}, u32[]{:S(2)}, u32[]{:S(2)}) collective-permute-start(bf16[8,8,3456]{2,1,0:T(8,128)(2,1)S(1)} %copy-done.13), channel_id=1, source_target_pairs={{0,3},{1,4},{2,5},{3,6},{4,7},{5,8},{6,9},{7,10},{8,11},{9,12},{10... | collective-permute-start | bytes 1327112 | tf_op jit(solution)/shard_map/ppermute | solution.py:22
  350.6 39.3 %all-to-all-start.3 = ((bf16[4,2,384,384]{3,2,1,0:T(8,128)(2,1)}), bf16[4,2,384,384]{3,2,1,0:T(8,128)(2,1)S(1)}, u32[]{:S(2)}, u32[]{:S(2)}) async-start(bf16[4,2,384,384]{3,2,1,0:T(8,128)(2,1)} %add_convert_fusion), calls=%async_computation.3 | async-start | bytes 4718592 | tf_op jit(solution)/shard_map/all_to_all | solution.py:318
  357.6 62.1 %collective-permute-start = (f32[4,128]{1,0:T(4,128)S(1)}, f32[4,128]{1,0:T(4,128)S(1)}, u32[]{:S(2)}, u32[]{:S(2)}) collective-permute-start(f32[4,128]{1,0:T(4,128)S(1)} %pad_maximum_fusion.7), channel_id=1, source_target_pairs={{0,768},{256,0},{512,256},{768,512},{1,769},{257,1},{513,257},{769... | collective-permute-start | bytes 6152 | tf_op jit(solution)/shard_map/ppermute | solution.py:22
  362.5 93.0 %collective-permute-start.16 = (bf16[4,8,3584]{2,1,0:T(8,128)(2,1)}, bf16[4,8,3584]{2,1,0:T(8,128)(2,1)}, u32[]{:S(2)}, u32[]{:S(2)}) collective-permute-start(bf16[4,8,3584]{2,1,0:T(8,128)(2,1)} %get-tuple-element.37), channel_id=1, source_target_pairs={{0,771},{1,772},{2,773},{3,774},{4,775},{5,776},{6,777},{7,778},{8... | collective-permute-start | bytes 688136 | tf_op jit(solution)/shard_map/ppermute | solution.py:32
  364.4 95.4 %collective-permute-start.17 = (bf16[4,8,3584]{2,1,0:T(8,128)(2,1)}, bf16[4,8,3584]{2,1,0:T(8,128)(2,1)}, u32[]{:S(2)}, u32[]{:S(2)}) collective-permute-start(bf16[4,8,3584]{2,1,0:T(8,128)(2,1)} %get-tuple-element.38), channel_id=1, source_target_pairs={{0,770},{1,771},{2,772},{3,773},{4,774},{5,775},{6,776},{7,777},{8... | collective-permute-start | bytes 688136 | tf_op jit(solution)/shard_map/ppermute | solution.py:32
  377.2 39.4 %collective-permute-start.29 = (bf16[192,384]{1,0:T(8,128)(2,1)}, bf16[192,384]{1,0:T(8,128)(2,1)}, u32[]{:S(2)}, u32[]{:S(2)}) collective-permute-start(bf16[192,384]{1,0:T(8,128)(2,1)} %get-tuple-element.60), channel_id=1, source_target_pairs={{0,24},{1,25},{2,26},{3,27},{4,28},{5,29},{6,30},{7,31},{8,0},{9,1... | collective-permute-start | bytes 442376 | tf_op jit(solution)/shard_map/ppermute | solution.py:22
  389.8 145.9 %all-to-all-start.2 = ((bf16[4,1,384,384]{3,2,1,0:T(8,128)(2,1)}), bf16[4,1,384,384]{3,2,1,0:T(8,128)(2,1)S(1)}, u32[]{:S(2)}, u32[]{:S(2)}) async-start(bf16[4,1,384,384]{3,2,1,0:T(8,128)(2,1)} %add_convert_fusion.2), calls=%async_computation.2 | async-start | bytes 2359296 | tf_op jit(solution)/shard_map/all_to_all | solution.py:318
  403.0 59.5 %collective-permute-start.18 = (bf16[4,8,3584]{2,1,0:T(8,128)(2,1)S(1)}, bf16[4,8,3584]{2,1,0:T(8,128)(2,1)S(1)}, u32[]{:S(2)}, u32[]{:S(2)}) collective-permute-start(bf16[4,8,3584]{2,1,0:T(8,128)(2,1)S(1)} %copy-done.21), channel_id=1, source_target_pairs={{0,769},{1,770},{2,771},{3,772},{4,773},{5,774},{6,775},{7,776},{8... | collective-permute-start | bytes 688136 | tf_op jit(solution)/shard_map/ppermute | solution.py:32
  419.7 56.4 %collective-permute-start.19 = (bf16[4,8,3584]{2,1,0:T(8,128)(2,1)S(1)}, bf16[4,8,3584]{2,1,0:T(8,128)(2,1)S(1)}, u32[]{:S(2)}, u32[]{:S(2)}) collective-permute-start(bf16[4,8,3584]{2,1,0:T(8,128)(2,1)S(1)} %copy-done.20), channel_id=1, source_target_pairs={{0,768},{1,769},{2,770},{3,771},{4,772},{5,773},{6,774},{7,775},{8... | collective-permute-start | bytes 688136 | tf_op jit(solution)/shard_map/ppermute | solution.py:32
  442.4 36.2 %collective-permute-start.20 = (bf16[4,8,3584]{2,1,0:T(8,128)(2,1)S(1)}, bf16[4,8,3584]{2,1,0:T(8,128)(2,1)S(1)}, u32[]{:S(2)}, u32[]{:S(2)}) collective-permute-start(bf16[4,8,3584]{2,1,0:T(8,128)(2,1)S(1)} %copy-done.19), channel_id=1, source_target_pairs={{0,799},{1,768},{2,769},{3,770},{4,771},{5,772},{6,773},{7,774},{8... | collective-permute-start | bytes 688136 | tf_op jit(solution)/shard_map/ppermute | solution.py:32
  459.9 66.1 %collective-permute-start.22 = (bf16[4,8,3584]{2,1,0:T(8,128)(2,1)S(1)}, bf16[4,8,3584]{2,1,0:T(8,128)(2,1)S(1)}, u32[]{:S(2)}, u32[]{:S(2)}) collective-permute-start(bf16[4,8,3584]{2,1,0:T(8,128)(2,1)S(1)} %copy-done.17), channel_id=1, source_target_pairs={{0,797},{1,798},{2,799},{3,768},{4,769},{5,770},{6,771},{7,772},{8... | collective-permute-start | bytes 688136 | tf_op jit(solution)/shard_map/ppermute | solution.py:32
  462.5 73.3 %collective-permute-start.28 = (bf16[384,384]{1,0:T(8,128)(2,1)S(1)}, bf16[384,384]{1,0:T(8,128)(2,1)S(1)}, u32[]{:S(2)}, u32[]{:S(2)}) collective-permute-start(bf16[384,384]{1,0:T(8,128)(2,1)S(1)} %pad_maximum_fusion.5), channel_id=1, source_target_pairs={{0,8},{1,9},{2,10},{3,11},{4,12},{5,13},{6,14},{7,15},{8,16},{9,17... | collective-permute-start | bytes 884744 | tf_op jit(solution)/shard_map/ppermute | solution.py:22
  476.1 72.0 %collective-permute-start.30 = (bf16[384,384]{1,0:T(8,128)(2,1)}, bf16[384,384]{1,0:T(8,128)(2,1)S(1)}, u32[]{:S(2)}, u32[]{:S(2)}) collective-permute-start(bf16[384,384]{1,0:T(8,128)(2,1)} %pad_maximum_fusion.6), channel_id=1, source_target_pairs={{0,24},{1,25},{2,26},{3,27},{4,28},{5,29},{6,30},{7,31},{8,0},{9,1... | collective-permute-start | bytes 884744 | tf_op jit(solution)/shard_map/ppermute | solution.py:22
  (37 other events, 1249.3 us)

commit v4 on v3

--- a/solution.py
+++ b/solution.py
@@ -20,16 +20,6 @@
 def shifted(value, axis, steps):
     count = lax.axis_size(axis)
     return lax.ppermute(value, axis, [(s, (s + steps) % count) for s in range(count)])
-
-
-def sent_back(value, steps):
-    sections, count = lax.axis_size("section"), lax.axis_size("expert")
-    pairs = [
-        (s * count + e, (s - 1) % sections * count + (e + steps) % count)
-        for s in range(sections)
-        for e in range(count)
-    ]
-    return lax.ppermute(value, ("section", "expert"), pairs)
 
 
 def offsets_of(reach):
@@ -134,18 +124,24 @@
     core_ref, refs = refs[0], refs[1:]
     arrived = refs[: len(offsets)]
     own_w = refs[len(offsets) : len(offsets) + 3]
-    side_w, far_w = refs[len(offsets) + 3 : len(offsets) + 5]
+    side_hbm, far_hbm = refs[len(offsets) + 3 : len(offsets) + 5]
     at = len(offsets) + 5
     returned = refs[at : at + len(offsets)]
     at += len(offsets)
     far_keep, far_give, side_keep, side_give, own_keep, own_give = refs[at : at + 6]
-    x_ref, g_ref, folded = refs[at + 6 :]
+    x_ref, g_ref, folded, side_w, far_w, term_ref, in_sems, out_sems = refs[at + 6 :]
+    far_in = pltpu.make_async_copy(far_hbm, far_w, in_sems.at[0])
+    side_in = pltpu.make_async_copy(side_hbm, side_w, in_sems.at[1])
+    far_in.start()
+    side_in.start()
+    core = core_ref[0]
+    flights = []
     width = own_w[0].shape[0]
     ff = own_w[0].shape[1]
     fold = width // SUB
     by_hidden = (((1,), (1,)), ((), ()))
     by_rows = (((0,), (0,)), ((), ()))
-    for k in range(COPIES):
+    for k in (0, 2, 1, 3):
         here = [(d, hosts_of(d, reach).index(k)) for d in offsets if k in hosts_of(d, reach)]
         count = len(here)
         padded = -(-count // SUB) * SUB
@@ -160,8 +156,11 @@
         if k == 0:
             gate_w, up_w, down_w = [w[...] for w in own_w]
         elif k == 2:
+            far_in.wait()
             gate_w, up_w, down_w = [far_w[:, :, 0, i].reshape(width, ff) for i in range(3)]
         else:
+            if k == 1:
+                side_in.wait()
             gate_w, up_w, down_w = [side_w[:, :, k // 2, i].reshape(width, ff) for i in range(3)]
         x = x_ref[0:rows, :]
         g = g_ref[0:rows, :]
@@ -198,18 +197,19 @@
         for i, (left, right) in enumerate(((x, d_gate), (x, d_up), (g, hidden))):
             cols = slice(i * ff, (i + 1) * ff)
             term = lax.dot_general(left, right, by_rows, preferred_element_type=F32).astype(BF16)
-            chips = far_keep.shape[0]
-            term = term.reshape(chips, CORES, -1, ff)
-            at = k // 2 if k % 2 else 0
-            keep, give = ((own_keep, own_give), (side_keep, side_give), (far_keep, far_give))[
-                1 if k % 2 else k
-            ]
-            for core in range(CORES):
-
-                @pl.when(core_ref[0] == core)
-                def _(term=term, core=core, keep=keep, give=give, at=at, cols=cols):
-                    keep[:, at, :, cols] = term[:, core]
-                    give[:, at, :, cols] = term[:, 1 - core]
+            term_ref[k, :, :, :, cols] = term.reshape(term_ref.shape[1:4] + (ff,))
+        keep, give = ((own_keep, own_give), (side_keep, side_give), (far_keep, far_give))[
+            1 if k % 2 else k
+        ]
+        to = k // 2 if k % 2 else 0
+        flights += [
+            pltpu.make_async_copy(term_ref.at[k, :, core], keep.at[:, to], out_sems.at[k, 0]),
+            pltpu.make_async_copy(term_ref.at[k, :, 1 - core], give.at[:, to], out_sems.at[k, 1]),
+        ]
+        for flight in flights[-2:]:
+            flight.start()
+    for flight in flights:
+        flight.wait()
 
 
 def run_experts(core, arrived, own_w, side_w, far_w, experts):
@@ -218,6 +218,7 @@
     fold = width // SUB
     chips = far_w.shape[1]
     vmem = pl.BlockSpec(memory_space=pltpu.VMEM)
+    anywhere = pl.BlockSpec(memory_space=pl.ANY)
     shapes = [
         jax.ShapeDtypeStruct((len(blocks_of(d, reach)), SUB, width + fold + EXTRA), BF16)
         for d in offsets_of(reach)
@@ -230,12 +231,19 @@
     outs = pl.pallas_call(
         lambda *refs: expert_kernel(*refs, experts=experts),
         out_shape=shapes,
-        in_specs=[pl.BlockSpec(memory_space=pltpu.SMEM)] + [vmem] * (len(arrived) + 5),
-        out_specs=[vmem] * len(shapes),
+        in_specs=[pl.BlockSpec(memory_space=pltpu.SMEM)]
+        + [vmem] * (len(arrived) + 3)
+        + [anywhere] * 2,
+        out_specs=[vmem] * len(arrived) + [anywhere] * 6,
         scratch_shapes=[
             pltpu.VMEM((rows, width), BF16),
             pltpu.VMEM((rows, width), BF16),
             pltpu.VMEM((count * SUB, fold), BF16),
+            pltpu.VMEM(side_w.shape, BF16),
+            pltpu.VMEM(far_w.shape, BF16),
+            pltpu.VMEM((COPIES, chips, CORES, width // (CORES * chips), 3 * ff), BF16),
+            pltpu.SemaphoreType.DMA((2,)),
+            pltpu.SemaphoreType.DMA((COPIES, 2)),
         ],
         name="experts",
         interpret=INTERPRET,
@@ -243,24 +251,10 @@
     return outs[:-6], outs[-6:]
 
 
-def scalars_kernel(here_ref, routes_ref, combine_ref, *refs, experts):
+def unpack_kernel(here_ref, routes_ref, combine_ref, *refs, experts):
     reach = experts // (2 * COPIES)
     offsets = offsets_of(reach)
-    combine_out, extra = refs[len(offsets) :]
-    for d, ref in zip(offsets, refs):
-        for i, b in enumerate(blocks_of(d, reach)):
-            extra[b * SUB : (b + 1) * SUB, :] = ref[i].astype(F32)
-    main, ninth, sub = selectors(routes_ref, here_ref[0], experts)
-    for k in range(2):
-        value = main[k] * extra[:, 0:1] + jnp.where(sub == 0, ninth[k], 0.0) * extra[:, 1:2]
-        value = jnp.sum(value, axis=0, keepdims=True)
-        combine_out[k : k + 1, :] = value / combine_ref[k : k + 1, :]
-
-
-def unpack_kernel(here_ref, routes_ref, *refs, experts):
-    reach = experts // (2 * COPIES)
-    offsets = offsets_of(reach)
-    grad_out, body, tail = refs[len(offsets) :]
+    grad_out, combine_out, body, tail, extra = refs[len(offsets) :]
     width = body.shape[1]
     fold = tail.shape[1]
     for d, ref in zip(offsets, refs):
@@ -268,6 +262,7 @@
             span = slice(b * SUB, (b + 1) * SUB)
             body[span, :] = ref[i, :, 0:width]
             tail[span, :] = ref[i, :, width : width + fold]
+            extra[span, :] = ref[i, :, width + fold : width + fold + EXTRA].astype(F32)
     main, ninth, sub = selectors(routes_ref, here_ref[0], experts)
     pick = (main[0] + main[1]).T.astype(BF16)
     nine = ninth[0] + ninth[1]
@@ -278,38 +273,31 @@
             jnp.where(sub == s, nine, 0.0).T.astype(BF16), tail[...], preferred_element_type=F32
         )
         grad_out[:, cols] = total.astype(BF16)
-
-
-def unpack_scalars(here, routes_t, combine_t, arrived, width, experts):
-    vmem = pl.BlockSpec(memory_space=pltpu.VMEM)
-    at = (width + width // SUB) // EXTRA
-    lanes = [pl.BlockSpec((a.shape[0], SUB, EXTRA), lambda i: (0, 0, at)) for a in arrived]
-    return pl.pallas_call(
-        lambda *refs: scalars_kernel(*refs, experts=experts),
-        grid=(1,),
-        out_shape=jax.ShapeDtypeStruct(routes_t.shape, F32),
-        in_specs=[pl.BlockSpec(memory_space=pltpu.SMEM), vmem, vmem] + lanes,
-        out_specs=vmem,
-        scratch_shapes=[pltpu.VMEM((experts * SUB, EXTRA), F32)],
-        name="scalars",
-        interpret=INTERPRET,
-    )(here, routes_t, combine_t, *arrived)
-
-
-def unpack(here, routes_t, arrived, width, experts):
+    for k in range(2):
+        value = main[k] * extra[:, 0:1] + jnp.where(sub == 0, ninth[k], 0.0) * extra[:, 1:2]
+        value = jnp.sum(value, axis=0, keepdims=True)
+        combine_out[k : k + 1, :] = value / combine_ref[k : k + 1, :].astype(F32)
+
+
+def unpack(here, routes_t, combine_t, arrived, width, experts):
+    tokens = routes_t.shape[1]
     vmem = pl.BlockSpec(memory_space=pltpu.VMEM)
     return pl.pallas_call(
         lambda *refs: unpack_kernel(*refs, experts=experts),
-        out_shape=jax.ShapeDtypeStruct((routes_t.shape[1], width), BF16),
-        in_specs=[pl.BlockSpec(memory_space=pltpu.SMEM)] + [vmem] * (1 + len(arrived)),
-        out_specs=vmem,
+        out_shape=[
+            jax.ShapeDtypeStruct((tokens, width), BF16),
+            jax.ShapeDtypeStruct((2, tokens), F32),
+        ],
+        in_specs=[pl.BlockSpec(memory_space=pltpu.SMEM)] + [vmem] * (2 + len(arrived)),
+        out_specs=[vmem] * 2,
         scratch_shapes=[
             pltpu.VMEM((experts * SUB, width), BF16),
             pltpu.VMEM((experts * SUB, width // SUB), BF16),
+            pltpu.VMEM((experts * SUB, EXTRA), F32),
         ],
         name="unpack",
         interpret=INTERPRET,
-    )(here, routes_t, *arrived)
+    )(here, routes_t, combine_t, *arrived)
 
 
 def over_chips(x):
@@ -358,7 +346,6 @@
     side_w = spread(jnp.stack([side1, side3]))
     far_w = spread(jnp.concatenate([low, high], axis=1)[None])
     packed = pack(here, routes_t, combine_t, tokens_in[0], upstream[0], experts)
-    behind = shifted(jnp.concatenate([routes_t.astype(F32), combine_t.astype(F32)]), "section", -1)
     arrived = list(packed)
     for i, d in enumerate(offsets):
         if d:
@@ -366,9 +353,10 @@
     done, terms = run_experts(
         core.reshape(1), arrived, own_w, side_w, far_w, experts
     )
-    back = []
+    back = list(done)
     for i, d in enumerate(offsets):
-        back.append(sent_back(done[i], -d))
+        if d:
+            back[i] = shifted(done[i], "expert", -d)
 
     def summed(keep, give):
         got = other_core(give)
@@ -385,11 +373,9 @@
     joined = jnp.concatenate([side_sum[1, : part // 2], side_sum[1, part // 2 :] + high.astype(F32)])
     side3 = shifted(joined.astype(BF16), "expert", -period)
     weight_grad = (own_sum + side1.astype(F32) + side3.astype(F32)) * (1.0 / replicas)
-    routes_b = behind[:2].astype(jnp.int32)
-    combine_grad = unpack_scalars(here, routes_b, behind[2:], back, width, experts)
-    combine_grad = shifted(combine_grad, "section", 1)
-    prev_grad = unpack(here, routes_b, back, width, experts)
-    return prev_grad[None], weight_grad[None, None], combine_grad.astype(BF16).T[None]
+    token_grad, combine_grad = unpack(here, routes_t, combine_t, back, width, experts)
+    prev_grad = shifted(token_grad[None], "section", -1)
+    return prev_grad, weight_grad[None, None], combine_grad.astype(BF16).T[None]
 
 
 def solution(mesh):

time: 551 us -> 503 us (0.913)
  the two profiles are of different devices: /device:TPU:2 before, /device:TPU:130 now
where the time goes in v4:
time: 503 us; the launch traced here: 501 us
  waiting for transfers between devices  260 us (52%)
  starting transfers between devices  187 us (37%)
  Pallas kernels  23 us (5%)
  other arithmetic  21.1 us (4%)
  local copies, waits for them, and re-layouts  8.89 us (2%)
    ppermute x25, waiting for transfers between devices, shifted(): lax.ppermute(value, axis, [(s, (s + steps) % count) for s in range(count)])  231 us
    ppermute x25, starting transfers between devices, shifted(): lax.ppermute(value, axis, [(s, (s + steps) % count) for s in range(count)])  152 us
    all_to_all x5, waiting for transfers between devices, over_chips(): lax.all_to_all(x, 'dp', split_axis=0, concat_axis=0, tiled=True, axis_ind...  25.1 us
    all_to_all x5, starting transfers between devices, over_chips(): lax.all_to_all(x, 'dp', split_axis=0, concat_axis=0, tiled=True, axis_ind...  24.4 us
    pallas_call x1, Pallas kernels, run_experts(): pl.pallas_call(lambda *refs: expert_kernel(*refs, experts=experts), out_s...  14.4 us
  transfers between devices with their start and end apart: 35, of which 19 were waited for; matrix products, arithmetic and copies ran while one was open for 4% of the time, Pallas kernels for 2%

profile of v4, /device:TPU:130, one launch (start us, length us, event | category | flops | bytes accessed | tf_op | source)
XLA Modules:
  0.0 500.9 jit_solution(14311038746123209271)
XLA Ops:
  2.6 15.7 %collective-permute-start.9 = (bf16[3,384,128]{2,1,0:T(8,128)(2,1)S(1)}, bf16[3,384,128]{2,1,0:T(8,128)(2,1)S(1)}, u32[]{:S(2)}, u32[]{:S(2)}) collective-permute-start(bf16[3,384,128]{2,1,0:T(8,128)(2,1)S(1)} %pad_maximum_fusion.3), channel_id=1, source_target_pairs={{0,8},{1,9},{2,10},{3,11},{4,12},{5,13},{6,14},{7,15},{8,16},{9,17... | collective-permute-start | bytes 884744 | tf_op jit(solution)/shard_map/ppermute | solution.py:22
  22.7 41.8 %collective-permute-done.9 = bf16[3,384,128]{2,1,0:T(8,128)(2,1)S(1)} collective-permute-done((bf16[3,384,128]{2,1,0:T(8,128)(2,1)S(1)}, bf16[3,384,128]{2,1,0:T(8,128)(2,1)S(1)}, u32[]{:S(2)}, u32[]{:S(2)}) %collective-permute-start.9) | collective-permute-done | bytes 294944 | tf_op jit(solution)/shard_map/ppermute | solution.py:22
  64.5 8.3 %collective-permute-done.8 = bf16[3,384,128]{2,1,0:T(8,128)(2,1)S(1)} collective-permute-done((bf16[3,384,128]{2,1,0:T(8,128)(2,1)S(1)}, bf16[3,384,128]{2,1,0:T(8,128)(2,1)S(1)}, u32[]{:S(2)}, u32[]{:S(2)}) %collective-permute-start.8) | collective-permute-done | bytes 294944 | tf_op jit(solution)/shard_map/ppermute | solution.py:22
  79.6 8.6 %collective-permute-start.12 = (bf16[3,192,128]{2,1,0:T(8,128)(2,1)S(1)}, bf16[3,192,128]{2,1,0:T(8,128)(2,1)S(1)}, u32[]{:S(2)}, u32[]{:S(2)}) collective-permute-start(bf16[3,192,128]{2,1,0:T(8,128)(2,1)S(1)} %slice.35), channel_id=1, source_target_pairs={{0,8},{1,9},{2,10},{3,11},{4,12},{5,13},{6,14},{7,15},{8,16},{9,17... | collective-permute-start | bytes 442376 | tf_op jit(solution)/shard_map/ppermute | solution.py:22
  94.2 16.6 %collective-permute-done.12 = bf16[3,192,128]{2,1,0:T(8,128)(2,1)S(1)} collective-permute-done((bf16[3,192,128]{2,1,0:T(8,128)(2,1)S(1)}, bf16[3,192,128]{2,1,0:T(8,128)(2,1)S(1)}, u32[]{:S(2)}, u32[]{:S(2)}) %collective-permute-start.12) | collective-permute-done | bytes 147488 | tf_op jit(solution)/shard_map/ppermute | solution.py:22
  124.4 13.2 %all-to-all-done.1 = bf16[4,1,3,384,128]{4,3,2,1,0:T(8,128)(2,1)S(1)} async-done(((bf16[4,1,3,384,128]{4,3,2,1,0:T(8,128)(2,1)}), bf16[4,1,3,384,128]{4,3,2,1,0:T(8,128)(2,1)S(1)}, u32[]{:S(2)}, u32[]{:S(2)}) %all-to-all-start.1) | async-done | bytes 1179680 | tf_op jit(solution)/shard_map/all_to_all | solution.py:306
  144.6 14.8 %collective-permute-start = (bf16[4,8,3456]{2,1,0:T(8,128)(2,1)}, bf16[4,8,3456]{2,1,0:T(8,128)(2,1)}, u32[]{:S(2)}, u32[]{:S(2)}) collective-permute-start(bf16[4,8,3456]{2,1,0:T(8,128)(2,1)} %get-tuple-element.29), channel_id=1, source_target_pairs={{0,28},{1,29},{2,30},{3,31},{4,0},{5,1},{6,2},{7,3},{8,4},{9,5},{1... | collective-permute-start | bytes 663560 | tf_op jit(solution)/shard_map/ppermute | solution.py:22
  170.4 7.4 %collective-permute-done.refs_1_ = bf16[4,8,3456]{2,1,0:T(8,128)(2,1)} collective-permute-done((bf16[4,8,3456]{2,1,0:T(8,128)(2,1)}, bf16[4,8,3456]{2,1,0:T(8,128)(2,1)}, u32[]{:S(2)}, u32[]{:S(2)}) %collective-permute-start) | collective-permute-done | bytes 221216 | tf_op jit(solution)/shard_map/ppermute | solution.py:22
  183.6 28.5 %collective-permute-done.1.refs_2_ = bf16[8,8,3456]{2,1,0:T(8,128)(2,1)} collective-permute-done((bf16[8,8,3456]{2,1,0:T(8,128)(2,1)}, bf16[8,8,3456]{2,1,0:T(8,128)(2,1)}, u32[]{:S(2)}, u32[]{:S(2)}) %collective-permute-start.1) | collective-permute-done | bytes 442400 | tf_op jit(solution)/shard_map/ppermute | solution.py:22
  221.6 7.8 %collective-permute-done.3.refs_4_ = bf16[8,8,3456]{2,1,0:T(8,128)(2,1)S(1)} collective-permute-done((bf16[8,8,3456]{2,1,0:T(8,128)(2,1)S(1)}, bf16[8,8,3456]{2,1,0:T(8,128)(2,1)S(1)}, u32[]{:S(2)}, u32[]{:S(2)}) %collective-permute-start.3) | collective-permute-done | bytes 442400 | tf_op jit(solution)/shard_map/ppermute | solution.py:22
  229.4 20.8 %collective-permute-done.5.refs_7_ = bf16[8,8,3456]{2,1,0:T(8,128)(2,1)} collective-permute-done((bf16[8,8,3456]{2,1,0:T(8,128)(2,1)S(1)}, bf16[8,8,3456]{2,1,0:T(8,128)(2,1)}, u32[]{:S(2)}, u32[]{:S(2)}) %collective-permute-start.5) | collective-permute-done | bytes 442400 | tf_op jit(solution)/shard_map/ppermute | solution.py:22
  250.2 14.4 %experts.1 = (bf16[2,8,3584]{2,1,0:T(8,128)(2,1)}, bf16[4,8,3584]{2,1,0:T(8,128)(2,1)}, bf16[4,8,3584]{2,1,0:T(8,128)(2,1)}, bf16[4,8,3584]{2,1,0:T(8,128)(2,1)}...) custom-call(s32[1]{0:T(128)} %bitcast.5.refs_0_, ...), custom_call_target="tpu_custom_call" | custom-call | tf_op jit(solution)/shard_map/experts/pallas_call | solution.py:231
  284.4 11.9 %all-to-all-done.4 = bf16[4,1,384,384]{3,2,1,0:T(8,128)(2,1)S(1)} async-done(((bf16[4,1,384,384]{3,2,1,0:T(8,128)(2,1)}), bf16[4,1,384,384]{3,2,1,0:T(8,128)(2,1)S(1)}, u32[]{:S(2)}, u32[]{:S(2)}) %all-to-all-start.4) | async-done | bytes 1179680 | tf_op jit(solution)/shard_map/all_to_all | solution.py:306
  307.2 19.3 %collective-permute-start.16 = (bf16[4,8,3584]{2,1,0:T(8,128)(2,1)}, bf16[4,8,3584]{2,1,0:T(8,128)(2,1)}, u32[]{:S(2)}, u32[]{:S(2)}) collective-permute-start(bf16[4,8,3584]{2,1,0:T(8,128)(2,1)} %get-tuple-element.40), channel_id=1, source_target_pairs={{0,2},{1,3},{2,4},{3,5},{4,6},{5,7},{6,8},{7,9},{8,10},{9,11},{10,... | collective-permute-start | bytes 688136 | tf_op jit(solution)/shard_map/ppermute | solution.py:22
  328.4 7.8 %collective-permute-start.21 = (bf16[2,8,3584]{2,1,0:T(8,128)(2,1)}, bf16[2,8,3584]{2,1,0:T(8,128)(2,1)}, u32[]{:S(2)}, u32[]{:S(2)}) collective-permute-start(bf16[2,8,3584]{2,1,0:T(8,128)(2,1)} %get-tuple-element.46), channel_id=1, source_target_pairs={{0,28},{1,29},{2,30},{3,31},{4,0},{5,1},{6,2},{7,3},{8,4},{9,5},{1... | collective-permute-start | bytes 344072 | tf_op jit(solution)/shard_map/ppermute | solution.py:22
  336.3 13.9 %collective-permute-done.14.refs_3_ = bf16[2,8,3584]{2,1,0:T(8,128)(2,1)} collective-permute-done((bf16[2,8,3584]{2,1,0:T(8,128)(2,1)}, bf16[2,8,3584]{2,1,0:T(8,128)(2,1)}, u32[]{:S(2)}, u32[]{:S(2)}) %collective-permute-start.14) | collective-permute-done | bytes 114720 | tf_op jit(solution)/shard_map/ppermute | solution.py:22
  361.9 6.9 %collective-permute-done.18.refs_8_ = bf16[4,8,3584]{2,1,0:T(8,128)(2,1)} collective-permute-done((bf16[4,8,3584]{2,1,0:T(8,128)(2,1)}, bf16[4,8,3584]{2,1,0:T(8,128)(2,1)}, u32[]{:S(2)}, u32[]{:S(2)}) %collective-permute-start.18) | collective-permute-done | bytes 229408 | tf_op jit(solution)/shard_map/ppermute | solution.py:22
  368.8 9.9 %collective-permute-done.19.refs_9_ = bf16[4,8,3584]{2,1,0:T(8,128)(2,1)} collective-permute-done((bf16[4,8,3584]{2,1,0:T(8,128)(2,1)}, bf16[4,8,3584]{2,1,0:T(8,128)(2,1)}, u32[]{:S(2)}, u32[]{:S(2)}) %collective-permute-start.19) | collective-permute-done | bytes 229408 | tf_op jit(solution)/shard_map/ppermute | solution.py:22
  378.7 6.5 %collective-permute-done.20.refs_10_ = bf16[4,8,3584]{2,1,0:T(8,128)(2,1)} collective-permute-done((bf16[4,8,3584]{2,1,0:T(8,128)(2,1)}, bf16[4,8,3584]{2,1,0:T(8,128)(2,1)}, u32[]{:S(2)}, u32[]{:S(2)}) %collective-permute-start.20) | collective-permute-done | bytes 229408 | tf_op jit(solution)/shard_map/ppermute | solution.py:22
  399.1 9.2 %collective-permute-start.26 = (bf16[192,384]{1,0:T(8,128)(2,1)}, bf16[192,384]{1,0:T(8,128)(2,1)}, u32[]{:S(2)}, u32[]{:S(2)}) collective-permute-start(bf16[192,384]{1,0:T(8,128)(2,1)} %get-tuple-element.63), channel_id=1, source_target_pairs={{0,8},{1,9},{2,10},{3,11},{4,12},{5,13},{6,14},{7,15},{8,16},{9,17... | collective-permute-start | bytes 442376 | tf_op jit(solution)/shard_map/ppermute | solution.py:22
  422.7 10.9 %collective-permute-done.28 = bf16[192,384]{1,0:T(8,128)(2,1)} collective-permute-done((bf16[192,384]{1,0:T(8,128)(2,1)}, bf16[192,384]{1,0:T(8,128)(2,1)}, u32[]{:S(2)}, u32[]{:S(2)}) %collective-permute-start.28) | collective-permute-done | bytes 147488 | tf_op jit(solution)/shard_map/ppermute | solution.py:22
  434.7 8.0 %collective-permute-start.29 = (bf16[384,384]{1,0:T(8,128)(2,1)S(1)}, bf16[384,384]{1,0:T(8,128)(2,1)S(1)}, u32[]{:S(2)}, u32[]{:S(2)}) collective-permute-start(bf16[384,384]{1,0:T(8,128)(2,1)S(1)} %pad_maximum_fusion.6), channel_id=1, source_target_pairs={{0,24},{1,25},{2,26},{3,27},{4,28},{5,29},{6,30},{7,31},{8,0},{9,1... | collective-permute-start | bytes 884744 | tf_op jit(solution)/shard_map/ppermute | solution.py:22
  442.8 13.1 %collective-permute-start.27 = (bf16[384,384]{1,0:T(8,128)(2,1)S(1)}, bf16[384,384]{1,0:T(8,128)(2,1)S(1)}, u32[]{:S(2)}, u32[]{:S(2)}) collective-permute-start(bf16[384,384]{1,0:T(8,128)(2,1)S(1)} %pad_maximum_fusion.5), channel_id=1, source_target_pairs={{0,8},{1,9},{2,10},{3,11},{4,12},{5,13},{6,14},{7,15},{8,16},{9,17... | collective-permute-start | bytes 884744 | tf_op jit(solution)/shard_map/ppermute | solution.py:22
  456.6 41.3 %collective-permute-done.29 = bf16[384,384]{1,0:T(8,128)(2,1)S(1)} collective-permute-done((bf16[384,384]{1,0:T(8,128)(2,1)S(1)}, bf16[384,384]{1,0:T(8,128)(2,1)S(1)}, u32[]{:S(2)}, u32[]{:S(2)}) %collective-permute-start.29) | collective-permute-done | bytes 294944 | tf_op jit(solution)/shard_map/ppermute | solution.py:22
  (93 shorter events, 142.9 us)
Async XLA Ops:
  2.6 61.9 %collective-permute-start.9 = (bf16[3,384,128]{2,1,0:T(8,128)(2,1)S(1)}, bf16[3,384,128]{2,1,0:T(8,128)(2,1)S(1)}, u32[]{:S(2)}, u32[]{:S(2)}) collective-permute-start(bf16[3,384,128]{2,1,0:T(8,128)(2,1)S(1)} %pad_maximum_fusion.3), channel_id=1, source_target_pairs={{0,8},{1,9},{2,10},{3,11},{4,12},{5,13},{6,14},{7,15},{8,16},{9,17... | collective-permute-start | bytes 884744 | tf_op jit(solution)/shard_map/ppermute | solution.py:22
  18.3 54.4 %collective-permute-start.8 = (bf16[3,384,128]{2,1,0:T(8,128)(2,1)S(1)}, bf16[3,384,128]{2,1,0:T(8,128)(2,1)S(1)}, u32[]{:S(2)}, u32[]{:S(2)}) collective-permute-start(bf16[3,384,128]{2,1,0:T(8,128)(2,1)S(1)} %pad_maximum_fusion.3), channel_id=1, source_target_pairs={{0,24},{1,25},{2,26},{3,27},{4,28},{5,29},{6,30},{7,31},{8,0},{9,1... | collective-permute-start | bytes 884744 | tf_op jit(solution)/shard_map/ppermute | solution.py:22
  74.7 41.7 %all-to-all-start = ((bf16[4,2,3,384,128]{4,3,2,1,0:T(8,128)(2,1)}), bf16[4,2,3,384,128]{4,3,2,1,0:T(8,128)(2,1)S(1)}, u32[]{:S(2)}, u32[]{:S(2)}) async-start(bf16[4,2,3,384,128]{4,3,2,1,0:T(8,128)(2,1)} %broadcast_in_dim.20), calls=%async_computation | async-start | bytes 4718592 | tf_op jit(solution)/shard_map/all_to_all | solution.py:306
  79.6 31.2 %collective-permute-start.12 = (bf16[3,192,128]{2,1,0:T(8,128)(2,1)S(1)}, bf16[3,192,128]{2,1,0:T(8,128)(2,1)S(1)}, u32[]{:S(2)}, u32[]{:S(2)}) collective-permute-start(bf16[3,192,128]{2,1,0:T(8,128)(2,1)S(1)} %slice.35), channel_id=1, source_target_pairs={{0,8},{1,9},{2,10},{3,11},{4,12},{5,13},{6,14},{7,15},{8,16},{9,17... | collective-permute-start | bytes 442376 | tf_op jit(solution)/shard_map/ppermute | solution.py:22
  88.2 28.2 %collective-permute-start.11 = (bf16[3,192,128]{2,1,0:T(8,128)(2,1)S(1)}, bf16[3,192,128]{2,1,0:T(8,128)(2,1)S(1)}, u32[]{:S(2)}, u32[]{:S(2)}) collective-permute-start(bf16[3,192,128]{2,1,0:T(8,128)(2,1)S(1)} %slice.34), channel_id=1, source_target_pairs={{0,24},{1,25},{2,26},{3,27},{4,28},{5,29},{6,30},{7,31},{8,0},{9,1... | collective-permute-start | bytes 442376 | tf_op jit(solution)/shard_map/ppermute | solution.py:22
  122.5 91.6 %collective-permute-start.10 = (bf16[4,2,3,384,128]{4,3,2,1,0:T(8,128)(2,1)S(1)}, bf16[4,2,3,384,128]{4,3,2,1,0:T(8,128)(2,1)}, u32[]{:S(2)}, u32[]{:S(2)}) collective-permute-start(bf16[4,2,3,384,128]{4,3,2,1,0:T(8,128)(2,1)S(1)} %all-to-all-done), channel_id=1, source_target_pairs={{0,32},{32,0},{64,96},{96,64},{128,160},{160,128},{192,224},{224,1... | collective-permute-start | bytes 7077896 | tf_op jit(solution)/shard_map/ppermute | solution.py:312
  137.6 27.8 %collective-permute-start.13 = (bf16[4,1,3,384,128]{4,3,2,0,1:T(8,128)(2,1)S(1)}, bf16[4,1,3,384,128]{4,3,2,0,1:T(8,128)(2,1)}, u32[]{:S(2)}, u32[]{:S(2)}) collective-permute-start(bf16[4,1,3,384,128]{4,3,2,0,1:T(8,128)(2,1)S(1)} %bitcast.57), channel_id=1, source_target_pairs={{0,32},{32,0},{64,96},{96,64},{128,160},{160,128},{192,224},{224,1... | collective-permute-start | bytes 3538952 | tf_op jit(solution)/shard_map/ppermute | solution.py:312
  144.6 33.1 %collective-permute-start = (bf16[4,8,3456]{2,1,0:T(8,128)(2,1)}, bf16[4,8,3456]{2,1,0:T(8,128)(2,1)}, u32[]{:S(2)}, u32[]{:S(2)}) collective-permute-start(bf16[4,8,3456]{2,1,0:T(8,128)(2,1)} %get-tuple-element.29), channel_id=1, source_target_pairs={{0,28},{1,29},{2,30},{3,31},{4,0},{5,1},{6,2},{7,3},{8,4},{9,5},{1... | collective-permute-start | bytes 663560 | tf_op jit(solution)/shard_map/ppermute | solution.py:22
  161.4 50.8 %collective-permute-start.1 = (bf16[8,8,3456]{2,1,0:T(8,128)(2,1)}, bf16[8,8,3456]{2,1,0:T(8,128)(2,1)}, u32[]{:S(2)}, u32[]{:S(2)}) collective-permute-start(bf16[8,8,3456]{2,1,0:T(8,128)(2,1)} %get-tuple-element.30), channel_id=1, source_target_pairs={{0,29},{1,30},{2,31},{3,0},{4,1},{5,2},{6,3},{7,4},{8,5},{9,6},{10... | collective-permute-start | bytes 1327112 | tf_op jit(solution)/shard_map/ppermute | solution.py:22
  165.4 56.3 %collective-permute-start.2 = (bf16[8,8,3456]{2,1,0:T(8,128)(2,1)}, bf16[8,8,3456]{2,1,0:T(8,128)(2,1)}, u32[]{:S(2)}, u32[]{:S(2)}) collective-permute-start(bf16[8,8,3456]{2,1,0:T(8,128)(2,1)} %get-tuple-element.31), channel_id=1, source_target_pairs={{0,30},{1,31},{2,0},{3,1},{4,2},{5,3},{6,4},{7,5},{8,6},{9,7},{10,... | collective-permute-start | bytes 1327112 | tf_op jit(solution)/shard_map/ppermute | solution.py:22
  177.7 51.7 %collective-permute-start.3 = (bf16[8,8,3456]{2,1,0:T(8,128)(2,1)S(1)}, bf16[8,8,3456]{2,1,0:T(8,128)(2,1)S(1)}, u32[]{:S(2)}, u32[]{:S(2)}) collective-permute-start(bf16[8,8,3456]{2,1,0:T(8,128)(2,1)S(1)} %copy-done.6), channel_id=1, source_target_pairs={{0,31},{1,0},{2,1},{3,2},{4,3},{5,4},{6,5},{7,6},{8,7},{9,8},{10,9... | collective-permute-start | bytes 1327112 | tf_op jit(solution)/shard_map/ppermute | solution.py:22
  179.7 49.7 %collective-permute-start.4 = (bf16[8,8,3456]{2,1,0:T(8,128)(2,1)S(1)}, bf16[8,8,3456]{2,1,0:T(8,128)(2,1)S(1)}, u32[]{:S(2)}, u32[]{:S(2)}) collective-permute-start(bf16[8,8,3456]{2,1,0:T(8,128)(2,1)S(1)} %copy-done.5), channel_id=1, source_target_pairs={{0,1},{1,2},{2,3},{3,4},{4,5},{5,6},{6,7},{7,8},{8,9},{9,10},{10,1... | collective-permute-start | bytes 1327112 | tf_op jit(solution)/shard_map/ppermute | solution.py:22
  212.1 38.1 %collective-permute-start.5 = (bf16[8,8,3456]{2,1,0:T(8,128)(2,1)S(1)}, bf16[8,8,3456]{2,1,0:T(8,128)(2,1)}, u32[]{:S(2)}, u32[]{:S(2)}) collective-permute-start(bf16[8,8,3456]{2,1,0:T(8,128)(2,1)S(1)} %copy-done.4), channel_id=1, source_target_pairs={{0,2},{1,3},{2,4},{3,5},{4,6},{5,7},{6,8},{7,9},{8,10},{9,11},{10,... | collective-permute-start | bytes 1327112 | tf_op jit(solution)/shard_map/ppermute | solution.py:22
  214.1 36.1 %collective-permute-start.6 = (bf16[8,8,3456]{2,1,0:T(8,128)(2,1)S(1)}, bf16[8,8,3456]{2,1,0:T(8,128)(2,1)}, u32[]{:S(2)}, u32[]{:S(2)}) collective-permute-start(bf16[8,8,3456]{2,1,0:T(8,128)(2,1)S(1)} %copy-done.3), channel_id=1, source_target_pairs={{0,3},{1,4},{2,5},{3,6},{4,7},{5,8},{6,9},{7,10},{8,11},{9,12},{10... | collective-permute-start | bytes 1327112 | tf_op jit(solution)/shard_map/ppermute | solution.py:22
  296.3 117.3 %all-to-all-start.3 = ((bf16[4,2,384,384]{3,2,1,0:T(8,128)(2,1)}), bf16[4,2,384,384]{3,2,1,0:T(8,128)(2,1)S(1)}, u32[]{:S(2)}, u32[]{:S(2)}) async-start(bf16[4,2,384,384]{3,2,1,0:T(8,128)(2,1)} %add_convert_fusion), calls=%async_computation.3 | async-start | bytes 4718592 | tf_op jit(solution)/shard_map/all_to_all | solution.py:306
  301.4 92.1 %collective-permute-start.23 = (bf16[4,1,384,384]{3,2,1,0:T(8,128)(2,1)}, bf16[4,1,384,384]{3,2,1,0:T(8,128)(2,1)}, u32[]{:S(2)}, u32[]{:S(2)}) collective-permute-start(bf16[4,1,384,384]{3,2,1,0:T(8,128)(2,1)} %get-tuple-element.49), channel_id=1, source_target_pairs={{0,32},{32,0},{64,96},{96,64},{128,160},{160,128},{192,224},{224,1... | collective-permute-start | bytes 3538952 | tf_op jit(solution)/shard_map/ppermute | solution.py:312
  303.3 54.7 %collective-permute-start.15 = (bf16[4,8,3584]{2,1,0:T(8,128)(2,1)}, bf16[4,8,3584]{2,1,0:T(8,128)(2,1)}, u32[]{:S(2)}, u32[]{:S(2)}) collective-permute-start(bf16[4,8,3584]{2,1,0:T(8,128)(2,1)} %get-tuple-element.39), channel_id=1, source_target_pairs={{0,3},{1,4},{2,5},{3,6},{4,7},{5,8},{6,9},{7,10},{8,11},{9,12},{10... | collective-permute-start | bytes 688136 | tf_op jit(solution)/shard_map/ppermute | solution.py:22
  307.2 52.7 %collective-permute-start.16 = (bf16[4,8,3584]{2,1,0:T(8,128)(2,1)}, bf16[4,8,3584]{2,1,0:T(8,128)(2,1)}, u32[]{:S(2)}, u32[]{:S(2)}) collective-permute-start(bf16[4,8,3584]{2,1,0:T(8,128)(2,1)} %get-tuple-element.40), channel_id=1, source_target_pairs={{0,2},{1,3},{2,4},{3,5},{4,6},{5,7},{6,8},{7,9},{8,10},{9,11},{10,... | collective-permute-start | bytes 688136 | tf_op jit(solution)/shard_map/ppermute | solution.py:22
  328.4 27.6 %collective-permute-start.21 = (bf16[2,8,3584]{2,1,0:T(8,128)(2,1)}, bf16[2,8,3584]{2,1,0:T(8,128)(2,1)}, u32[]{:S(2)}, u32[]{:S(2)}) collective-permute-start(bf16[2,8,3584]{2,1,0:T(8,128)(2,1)} %get-tuple-element.46), channel_id=1, source_target_pairs={{0,28},{1,29},{2,30},{3,31},{4,0},{5,1},{6,2},{7,3},{8,4},{9,5},{1... | collective-permute-start | bytes 344072 | tf_op jit(solution)/shard_map/ppermute | solution.py:22
  359.9 25.3 %collective-permute-start.20 = (bf16[4,8,3584]{2,1,0:T(8,128)(2,1)}, bf16[4,8,3584]{2,1,0:T(8,128)(2,1)}, u32[]{:S(2)}, u32[]{:S(2)}) collective-permute-start(bf16[4,8,3584]{2,1,0:T(8,128)(2,1)} %get-tuple-element.45), channel_id=1, source_target_pairs={{0,29},{1,30},{2,31},{3,0},{4,1},{5,2},{6,3},{7,4},{8,5},{9,6},{10... | collective-permute-start | bytes 688136 | tf_op jit(solution)/shard_map/ppermute | solution.py:22
  388.7 67.7 %collective-permute-start.22 = (bf16[1,128,3072]{2,1,0:T(8,128)(2,1)}, bf16[1,128,3072]{2,1,0:T(8,128)(2,1)}, u32[]{:S(2)}, u32[]{:S(2)}) collective-permute-start(bf16[1,128,3072]{2,1,0:T(8,128)(2,1)} %bitcast.69), channel_id=1, source_target_pairs={{0,768},{256,0},{512,256},{768,512},{1,769},{257,1},{513,257},{769... | collective-permute-start | bytes 2359304 | tf_op jit(solution)/shard_map/ppermute | solution.py:22
  413.6 42.8 %all-to-all-start.2 = ((bf16[4,1,384,384]{3,2,1,0:T(8,128)(2,1)}), bf16[4,1,384,384]{3,2,1,0:T(8,128)(2,1)S(1)}, u32[]{:S(2)}, u32[]{:S(2)}) async-start(bf16[4,1,384,384]{3,2,1,0:T(8,128)(2,1)} %add_convert_fusion.2), calls=%async_computation.2 | async-start | bytes 2359296 | tf_op jit(solution)/shard_map/all_to_all | solution.py:306
  434.7 63.2 %collective-permute-start.29 = (bf16[384,384]{1,0:T(8,128)(2,1)S(1)}, bf16[384,384]{1,0:T(8,128)(2,1)S(1)}, u32[]{:S(2)}, u32[]{:S(2)}) collective-permute-start(bf16[384,384]{1,0:T(8,128)(2,1)S(1)} %pad_maximum_fusion.6), channel_id=1, source_target_pairs={{0,24},{1,25},{2,26},{3,27},{4,28},{5,29},{6,30},{7,31},{8,0},{9,1... | collective-permute-start | bytes 884744 | tf_op jit(solution)/shard_map/ppermute | solution.py:22
  442.8 55.1 %collective-permute-start.27 = (bf16[384,384]{1,0:T(8,128)(2,1)S(1)}, bf16[384,384]{1,0:T(8,128)(2,1)S(1)}, u32[]{:S(2)}, u32[]{:S(2)}) collective-permute-start(bf16[384,384]{1,0:T(8,128)(2,1)S(1)} %pad_maximum_fusion.5), channel_id=1, source_target_pairs={{0,8},{1,9},{2,10},{3,11},{4,12},{5,13},{6,14},{7,15},{8,16},{9,17... | collective-permute-start | bytes 884744 | tf_op jit(solution)/shard_map/ppermute | solution.py:22
  (19 other events, 396.0 us)
